TPU v7x, 512 devices: a whole 4x8x8 slice. The times are simulated.
512 devices in a mesh: ep: 16 (over z_hi, y), sp: 32 (over z_lo, x, core).
Axes of the slice: x: 4, y: 8, z: 8 (z_hi: 2, z_lo: 4; z = z_hi * 4 + z_lo), core: 2. Of those that a mesh axis runs over, the one named last changes fastest.
Arguments:
- grad_out: bfloat16 [65536, 4096], P(('ep', 'sp')), may hold values from -1.5 to 1.5
- routes: int32 [65536, 8], P(('ep', 'sp')), may hold values from 0 to 127, as said below
- gate: bfloat16 [65536, 8], P(('ep', 'sp')), may hold values from 0.049804688 to 1
- saved: bfloat16 [16, 32, 256, 3072], P('ep', 'sp'), may hold values from -6 to 6
- w_down: bfloat16 [16, 1536, 4096], P('ep', None, 'sp'), may hold values from -0.15625 to 0.15625
Outputs:
- grad_pre: bfloat16 [16, 32, 256, 3072], P('ep', 'sp')
- grad_gate: float32 [65536, 8], P(('ep', 'sp'))
Inputs may be any that keep to these rules, and one draw needn't show every extreme that they name: `routes`: each row names 8 different experts. In every block of 128 rows at most 16 rows name the same expert whose number is a multiple of 8, and in every block one such expert is named by exactly 16 rows; it is the same expert for all blocks whose indices agree modulo 32.
All inputs are finite; a program needn't handle non-finite values.
Results may differ from a plain program's by a relative error of at most 0.0029.
Values may be sent and summed in bfloat16 or wider, within the bound.
No kernel may reach another device: no remote copies, remote signals or barrier semaphores. Data moves between devices by JAX's collectives and lax.ppermute only.
A program may use at most 128 MiB of HBM per device.

v0:
```python
import functools

import jax
import jax.numpy as jnp
from jax import lax
from jax.experimental import pallas as pl
from jax.experimental.pallas import tpu as pltpu
from jax.sharding import Mesh, PartitionSpec as P


LANES = 128
STEP = 8
EP = ("zh", "y")
F32, BF16 = jnp.float32, jnp.bfloat16
VMEM = pl.BlockSpec(memory_space=pltpu.VMEM)
SMEM = pl.BlockSpec(memory_space=pltpu.SMEM)


def ring(size, shift):
    return [((i + shift) % size, i) for i in range(size)]


def pack_kernel(core_ref, tokens_ref, routes_ref, gate_ref, keep_ref, send_ref):
    core = core_ref[0]
    rows = tokens_ref.shape[0]
    table = jnp.concatenate(
        [routes_ref[...].astype(F32), gate_ref[...].astype(F32)], axis=0
    ).astype(BF16)
    for ref, parity in ((keep_ref, core), (send_ref, 1 - core)):
        for b in range(ref.shape[1] // LANES):
            start = pl.multiple_of((2 * b + parity) * LANES, LANES)
            ref[:rows, b * LANES : (b + 1) * LANES] = tokens_ref[:, pl.ds(start, LANES)]
        ref[rows:, :] = jnp.zeros((table.shape[0], ref.shape[1]), BF16)
        ref[rows:, :LANES] = table


def places(routes, experts):
    tokens = routes.shape[1]
    wanted = (STEP * lax.broadcasted_iota(jnp.int32, (experts, tokens), 0)).astype(F32)
    hits = [routes[k : k + 1, :] == wanted for k in range(routes.shape[0])]
    member = functools.reduce(jnp.add, [h.astype(F32) for h in hits])
    before = lax.broadcasted_iota(jnp.int32, (tokens, tokens), 0) < lax.broadcasted_iota(
        jnp.int32, (tokens, tokens), 1
    )
    place = lax.dot_general(
        member.astype(BF16),
        before.astype(F32).astype(BF16),
        (((1,), (0,)), ((), ())),
        preferred_element_type=F32,
    )
    return hits, jnp.where(member > 0.5, place, -1.0)


def one_hot(place, capacity):
    experts, tokens = place.shape
    spread = jnp.broadcast_to(place[:, None, :], (experts, capacity, tokens))
    slot = lax.broadcasted_iota(jnp.int32, (experts, capacity, tokens), 1).astype(F32)
    return (spread == slot).astype(F32).reshape(experts * capacity, tokens)


def eye(shape):
    return lax.broadcasted_iota(jnp.int32, shape, 1) == lax.broadcasted_iota(jnp.int32, shape, 2)


def to_lanes(column, sources):
    rows = column.shape[0]
    shape = (sources, rows // sources, LANES)
    spread = jnp.broadcast_to(column, (rows, LANES)).reshape(shape)
    return jnp.sum(jnp.where(eye(shape), spread, 0.0), axis=1, keepdims=True)


def to_column(line, capacity):
    sources = line.shape[0]
    shape = (sources, capacity, LANES)
    spread = jnp.where(eye(shape), jnp.broadcast_to(line, shape), 0.0)
    return jnp.sum(spread.reshape(sources * capacity, LANES), axis=1, keepdims=True)


def dispatch_kernel(core_ref, keep_ref, got_ref, out_ref):
    core = core_ref[0]
    experts = out_ref.shape[0]
    blocks = keep_ref.shape[1] // LANES
    capacity = (out_ref.shape[1] - 8) // (2 * blocks)
    tokens = LANES
    lines = [None, None]
    for which, (ref, side) in enumerate(((keep_ref, core), (got_ref, 1 - core))):
        table = ref[tokens:, :LANES].astype(F32)
        half = table.shape[0] // 2
        routes, gate = table[:half], table[half:]
        hits, place = places(routes, experts)
        gates = functools.reduce(
            jnp.add, [jnp.where(h, gate[k : k + 1, :], 0.0) for k, h in enumerate(hits)]
        )
        chosen = one_hot(place, capacity)
        spread = jnp.broadcast_to(gates[:, None, :], (experts, capacity, tokens))
        column = jnp.sum(
            chosen * spread.reshape(experts * capacity, tokens), axis=1, keepdims=True
        )
        lines[which] = to_lanes(column, experts)
        rows = jnp.dot(chosen.astype(BF16), ref[:tokens, :], preferred_element_type=F32)
        rows = rows.astype(BF16)
        for b in range(blocks):
            base = pl.multiple_of(2 * capacity * b + side * capacity, capacity)
            out_ref[:, pl.ds(base, capacity), :] = rows[:, b * LANES : (b + 1) * LANES].reshape(
                experts, capacity, LANES
            )
    tile = (experts, 8, LANES)
    first = lax.broadcasted_iota(jnp.int32, tile, 1) == core
    out_ref[:, 2 * capacity * blocks :, :] = jnp.where(
        first, jnp.broadcast_to(lines[0], tile), jnp.broadcast_to(lines[1], tile)
    ).astype(BF16)


def matmul_kernel(shifts, other, info_ref, arrived_ref, *refs):
    weights, (out_ref, rows_ref) = refs[:-2], refs[-2:]
    parts = [(w, i) for w in weights for i in range(w.shape[0])]

    @pl.when(pl.program_id(0) == 0)
    def _():
        side = 1 - info_ref[0] if other else info_ref[0]
        slots = out_ref.shape[0]
        capacity = slots // arrived_ref.shape[0]
        for n, (dz, dx) in enumerate(shifts):
            chip = ((info_ref[1] + dz) & 3) * 4 + ((info_ref[2] + dx) & 3)
            start = pl.multiple_of(2 * capacity * chip + capacity * side, capacity)
            rows_ref[:, n * LANES : (n + 1) * LANES] = arrived_ref[
                :, pl.ds(start, capacity), :
            ].reshape(slots, LANES)

    block = jnp.concatenate([w[i] for w, i in parts], axis=1)
    out_ref[...] = lax.dot_general(
        rows_ref[...], block, (((1,), (1,)), ((), ())), preferred_element_type=F32
    )


def finish_kernel(info_ref, mine_ref, theirs_ref, saved_ref, gate_ref, out_ref, score_ref):
    rows, units = mine_ref.shape
    here = pl.ds(pl.multiple_of(pl.program_id(0) * rows, rows), rows)
    sources = score_ref.shape[0]
    step = 256
    total = jnp.zeros((rows, 1), F32)
    tile = gate_ref[...].astype(F32)
    mine = lax.broadcasted_iota(jnp.int32, tile.shape, 1) == info_ref[0]
    line = jnp.sum(jnp.where(mine, tile, 0.0), axis=1, keepdims=True)
    gate_in = to_column(line, rows // sources)
    for j in range(units // step):
        cols = slice(j * step, (j + 1) * step)
        up_cols = slice(units + j * step, units + (j + 1) * step)
        grad = mine_ref[:, cols] + theirs_ref[here, cols]
        a = saved_ref[:, cols].astype(F32)
        u = saved_ref[:, up_cols].astype(F32)
        sig = 1.0 / (1.0 + jnp.exp(-a))
        silu = a * sig
        hidden = (silu * u).astype(BF16).astype(F32)
        total += jnp.sum(grad * hidden, axis=1, keepdims=True)
        scaled = grad * gate_in
        out_ref[:, cols] = (scaled * u * sig * (1.0 + a * (1.0 - sig))).astype(BF16)
        out_ref[:, up_cols] = (scaled * silu).astype(BF16)
    score_ref[...] = jnp.broadcast_to(to_lanes(total, sources), score_ref.shape)


def home_kernel(routes_ref, back_ref, out_ref):
    experts = back_ref.shape[0]
    routes = routes_ref[...].astype(F32)
    hits, place = places(routes, experts)
    chosen = one_hot(place, CAPACITY)
    column = to_column(back_ref[:, :1, :], CAPACITY)
    score = jnp.sum((column * chosen).reshape(experts, CAPACITY, -1), axis=1)
    for k, h in enumerate(hits):
        out_ref[k : k + 1, :] = jnp.sum(jnp.where(h, score, 0.0), axis=0, keepdims=True)


CAPACITY = 16


def call(kernel, shapes, in_specs, out_specs, scratch=(), grid=()):
    return pl.pallas_call(
        kernel,
        out_shape=shapes,
        grid=grid,
        in_specs=in_specs,
        out_specs=out_specs,
        scratch_shapes=list(scratch),
        compiler_params=pltpu.CompilerParams(vmem_limit_bytes=24 << 20),
    )


def near(array):
    return pltpu.with_memory_space_constraint(array, pltpu.VMEM)


def far(array):
    return pltpu.with_memory_space_constraint(array, pltpu.HBM)


def permute(array, axis, shift):
    return lax.ppermute(array, axis, ring(4, shift))


def gather_weights(block):
    z1, z3, z2 = (permute(block, "zl", r) for r in (1, 3, 2))
    first = [block] + [permute(block, "x", r) for r in (1, 3, 2)]
    pair = jnp.concatenate([z1, z3], axis=0)
    second = [pair] + [permute(pair, "x", r) for r in (1, 3, 2)]
    third = [z2] + [permute(z2, "x", r) for r in (1, 3, 2)]
    groups, shifts = [], []
    for arrays, zs in ((first, (0,)), (second, (1, 3)), (third, (2,))):
        for array, r in zip(arrays, (0, 1, 3, 2)):
            groups.append(array)
            shifts += [(dz, r) for dz in zs]
    return groups, shifts


def step(grad_out, routes, gate, saved, w_down):
    tokens, width = grad_out.shape
    units, slots = w_down.shape[1], saved.shape[2]
    sources = slots // CAPACITY
    groups, shifts = gather_weights(w_down)
    info = jnp.stack([lax.axis_index(a) for a in ("c", "zl", "x")]).astype(jnp.int32)
    half = width // 2
    blocks = half // LANES
    routes_t, gate_t = routes.T, gate.T
    packed = jax.ShapeDtypeStruct((tokens + 16, half), BF16)
    keep, send = call(pack_kernel, (packed, packed), [SMEM, VMEM, VMEM, VMEM], (VMEM, VMEM))(
        info, grad_out, routes_t, gate_t
    )
    got = lax.ppermute(send, "c", ring(2, 1))
    outgoing = call(
        dispatch_kernel,
        jax.ShapeDtypeStruct((sources, 2 * CAPACITY * blocks + 8, LANES), BF16),
        [SMEM, VMEM, VMEM],
        VMEM,
    )(info, keep, got)
    arrived = lax.all_to_all(outgoing, EP, split_axis=0, concat_axis=0, tiled=True)
    part = 256
    theirs, mine = (
        call(
            functools.partial(matmul_kernel, shifts, other),
            jax.ShapeDtypeStruct((slots, units), F32),
            [SMEM, VMEM]
            + [pl.BlockSpec((g.shape[0], part, LANES), lambda j: (0, j, 0)) for g in groups],
            pl.BlockSpec((slots, part), lambda j: (0, j)),
            [pltpu.VMEM((slots, half), BF16)],
            (units // part,),
        )(info, near(arrived), *map(far, groups))
        for other in (True, False)
    )
    theirs = lax.ppermute(theirs, "c", ring(2, 1))
    gates = arrived[:, 2 * CAPACITY * blocks :, :]
    steps = 4
    rows = slots // steps
    tile = pl.BlockSpec((sources // steps, 8, LANES), lambda i: (i, 0, 0))
    wide = pl.BlockSpec((rows, 2 * units), lambda i: (i, 0))
    grad_pre, score = call(
        finish_kernel,
        (
            jax.ShapeDtypeStruct((slots, 2 * units), BF16),
            jax.ShapeDtypeStruct((sources, 8, LANES), F32),
        ),
        [SMEM, pl.BlockSpec((rows, units), lambda i: (i, 0)), VMEM, wide, tile],
        (wide, tile),
        grid=(steps,),
    )(info, mine, near(theirs), saved[0, 0], gates)
    back = lax.all_to_all(score, EP, split_axis=0, concat_axis=0, tiled=True)
    grad_gate = call(
        home_kernel, jax.ShapeDtypeStruct((routes.shape[1], tokens), F32), [VMEM, VMEM], VMEM
    )(routes_t, back)
    return grad_pre.reshape(saved.shape), grad_gate.T


def solution(mesh):
    fine = Mesh(mesh.devices.reshape(2, 8, 4, 4, 2), ("zh", "y", "zl", "x", "c"))
    sp = ("zl", "x", "c")
    in_specs = (
        P(EP + sp, None),
        P(EP + sp, None),
        P(EP + sp, None),
        P(EP, sp, None, None),
        P(EP, None, sp),
    )
    out_specs = (P(EP, sp, None, None), P(EP + sp, None))
    return jax.shard_map(step, mesh=fine, in_specs=in_specs, out_specs=out_specs, check_vma=False)
```

profile of v0, /device:TPU:1, one launch (start us, length us, event | category | flops | bytes accessed | tf_op | source)
XLA Modules:
  0.0 214.8 jit_solution(12099617662440547887)
XLA Ops:
  0.6 0.1 pad_add_fusion.core_ref.info_ref
  0.7 1.2 copy-done.2
  1.9 0.7 copy-done.3
  2.6 0.7 copy-done.5
  3.3 0.8 shard_map.68
  4.1 8.7 %collective-permute-start = (bf16[144,2048]{1,0:T(8,128)(2,1)S(1)}, bf16[144,2048]{1,0:T(8,128)(2,1)S(1)}, u32[]{:S(2)}, u32[]{:S(2)}) collective-permute-start(bf16[144,2048]{1,0:T(8,128)(2,1)S(1)} %get-tuple-element.7), channel_id=1, source_target_pairs={{1,0},{0,1},{3,2},{2,3},{5,4},{4,5},{7,6},{6,7},{9,8},{8,9},{11,10... | collective-permute-start | bytes 1769480 | tf_op jit(solution)/shard_map/ppermute | solution.py:227
  12.9 1.6 collective-permute-done.got_ref
  14.5 1.6 shard_map.69
  16.1 1.3 copy-done
  17.4 10.2 %all-to-all-start = ((bf16[16,520,128]{2,1,0:T(8,128)(2,1)}), bf16[16,520,128]{2,1,0:T(8,128)(2,1)S(1)}, u32[]{:S(2)}, u32[]{:S(2)}) async-start(bf16[16,520,128]{2,1,0:T(8,128)(2,1)} %copy-done), calls=%async_computation | async-start | bytes 4259840 | tf_op jit(solution)/shard_map/all_to_all | solution.py:234
  27.6 4.9 %collective-permute-start.4 = (bf16[1,1536,128]{2,1,0:T(8,128)(2,1)S(1)}, bf16[1,1536,128]{2,1,0:T(8,128)(2,1)S(1)}, u32[]{:S(2)}, u32[]{:S(2)}) collective-permute-start(bf16[1,1536,128]{2,1,0:T(8,128)(2,1)S(1)} %copy-done.9), channel_id=1, source_target_pairs={{8,0},{16,8},{24,16},{0,24},{9,1},{17,9},{25,17},{1,25},{10,2},{18... | collective-permute-start | bytes 1179656 | tf_op jit(solution)/shard_map/ppermute | solution.py:197
  32.5 1.9 collective-permute-start.5
  34.4 4.4 %collective-permute-start.1 = (bf16[1,1536,128]{2,1,0:T(8,128)(2,1)S(1)}, bf16[1,1536,128]{2,1,0:T(8,128)(2,1)S(1)}, u32[]{:S(2)}, u32[]{:S(2)}) collective-permute-start(bf16[1,1536,128]{2,1,0:T(8,128)(2,1)S(1)} %copy-done.9), channel_id=1, source_target_pairs={{2,0},{4,2},{6,4},{0,6},{3,1},{5,3},{7,5},{1,7},{10,8},{12,10},{14... | collective-permute-start | bytes 1179656 | tf_op jit(solution)/shard_map/ppermute | solution.py:197
  38.8 1.9 collective-permute-start.2
  40.8 3.6 %collective-permute-start.3 = (bf16[1,1536,128]{2,1,0:T(8,128)(2,1)S(1)}, bf16[1,1536,128]{2,1,0:T(8,128)(2,1)S(1)}, u32[]{:S(2)}, u32[]{:S(2)}) collective-permute-start(bf16[1,1536,128]{2,1,0:T(8,128)(2,1)S(1)} %copy-done.9), channel_id=1, source_target_pairs={{4,0},{6,2},{0,4},{2,6},{5,1},{7,3},{1,5},{3,7},{12,8},{14,10},{8,... | collective-permute-start | bytes 1179656 | tf_op jit(solution)/shard_map/ppermute | solution.py:197
  44.4 42.5 %collective-permute-done.4 = bf16[1,1536,128]{2,1,0:T(8,128)(2,1)S(1)} collective-permute-done((bf16[1,1536,128]{2,1,0:T(8,128)(2,1)S(1)}, bf16[1,1536,128]{2,1,0:T(8,128)(2,1)S(1)}, u32[]{:S(2)}, u32[]{:S(2)}) %collective-permute-start.4) | collective-permute-done | bytes 393248 | tf_op jit(solution)/shard_map/ppermute | solution.py:197
  86.9 1.9 collective-permute-start.9
  88.8 6.6 %collective-permute-done.5 = bf16[1,1536,128]{2,1,0:T(8,128)(2,1)S(1)} collective-permute-done((bf16[1,1536,128]{2,1,0:T(8,128)(2,1)S(1)}, bf16[1,1536,128]{2,1,0:T(8,128)(2,1)S(1)}, u32[]{:S(2)}, u32[]{:S(2)}) %collective-permute-start.5) | collective-permute-done | bytes 393248 | tf_op jit(solution)/shard_map/ppermute | solution.py:197
  95.4 0.1 constant_dynamic-update-slice_fusion.refs_4_
  95.5 0.0 copy-start.6
  95.5 4.5 %collective-permute-start.6 = (bf16[2,1536,128]{2,1,0:T(8,128)(2,1)S(1)}, bf16[2,1536,128]{2,1,0:T(8,128)(2,1)S(1)}, u32[]{:S(2)}, u32[]{:S(2)}) collective-permute-start(bf16[2,1536,128]{2,1,0:T(8,128)(2,1)S(1)} %constant_dynamic-update-slice_fusion.refs_4_), channel_id=1, source_target_pairs={{2,0},{4,2},{6,4},{0,6},{3,1},{5,3},{7,5},{1,7},{10,8},{12,10},{14... | collective-permute-start | bytes 2359304 | tf_op jit(solution)/shard_map/ppermute | solution.py:197
  100.0 11.6 %collective-permute-done.9.refs_8_ = bf16[1,1536,128]{2,1,0:T(8,128)(2,1)S(1)} collective-permute-done((bf16[1,1536,128]{2,1,0:T(8,128)(2,1)S(1)}, bf16[1,1536,128]{2,1,0:T(8,128)(2,1)S(1)}, u32[]{:S(2)}, u32[]{:S(2)}) %collective-permute-start.9) | collective-permute-done | bytes 393248 | tf_op jit(solution)/shard_map/ppermute | solution.py:197
  111.7 4.4 %collective-permute-start.10 = (bf16[1,1536,128]{2,1,0:T(8,128)(2,1)S(1)}, bf16[1,1536,128]{2,1,0:T(8,128)(2,1)S(1)}, u32[]{:S(2)}, u32[]{:S(2)}) collective-permute-start(bf16[1,1536,128]{2,1,0:T(8,128)(2,1)S(1)} %collective-permute-done.9.refs_8_), channel_id=1, source_target_pairs={{2,0},{4,2},{6,4},{0,6},{3,1},{5,3},{7,5},{1,7},{10,8},{12,10},{14... | collective-permute-start | bytes 1179656 | tf_op jit(solution)/shard_map/ppermute | solution.py:197
  116.0 0.0 collective-permute-done.1.refs_1_
  116.1 1.9 collective-permute-start.7
  118.0 0.0 collective-permute-done.2.refs_2_
  118.0 3.6 %collective-permute-start.8 = (bf16[2,1536,128]{2,1,0:T(8,128)(2,1)S(1)}, bf16[2,1536,128]{2,1,0:T(8,128)(2,1)}, u32[]{:S(2)}, u32[]{:S(2)}) collective-permute-start(bf16[2,1536,128]{2,1,0:T(8,128)(2,1)S(1)} %constant_dynamic-update-slice_fusion.refs_4_), channel_id=1, source_target_pairs={{4,0},{6,2},{0,4},{2,6},{5,1},{7,3},{1,5},{3,7},{12,8},{14,10},{8,... | collective-permute-start | bytes 2359304 | tf_op jit(solution)/shard_map/ppermute | solution.py:197
  121.6 0.0 collective-permute-done.3.refs_3_
  121.7 3.4 %collective-permute-start.11 = (bf16[1,1536,128]{2,1,0:T(8,128)(2,1)S(1)}, bf16[1,1536,128]{2,1,0:T(8,128)(2,1)S(1)}, u32[]{:S(2)}, u32[]{:S(2)}) collective-permute-start(bf16[1,1536,128]{2,1,0:T(8,128)(2,1)S(1)} %collective-permute-done.9.refs_8_), channel_id=1, source_target_pairs={{6,0},{0,2},{2,4},{4,6},{7,1},{1,3},{3,5},{5,7},{14,8},{8,10},{10,... | collective-permute-start | bytes 1179656 | tf_op jit(solution)/shard_map/ppermute | solution.py:197
  125.1 16.6 %collective-permute-done.10.refs_9_ = bf16[1,1536,128]{2,1,0:T(8,128)(2,1)S(1)} collective-permute-done((bf16[1,1536,128]{2,1,0:T(8,128)(2,1)S(1)}, bf16[1,1536,128]{2,1,0:T(8,128)(2,1)S(1)}, u32[]{:S(2)}, u32[]{:S(2)}) %collective-permute-start.10) | collective-permute-done | bytes 393248 | tf_op jit(solution)/shard_map/ppermute | solution.py:197
  141.7 1.9 collective-permute-start.12
  143.6 20.1 %collective-permute-done.11.refs_10_ = bf16[1,1536,128]{2,1,0:T(8,128)(2,1)S(1)} collective-permute-done((bf16[1,1536,128]{2,1,0:T(8,128)(2,1)S(1)}, bf16[1,1536,128]{2,1,0:T(8,128)(2,1)S(1)}, u32[]{:S(2)}, u32[]{:S(2)}) %collective-permute-start.11) | collective-permute-done | bytes 393248 | tf_op jit(solution)/shard_map/ppermute | solution.py:197
  163.7 6.7 %collective-permute-done.12.refs_11_ = bf16[1,1536,128]{2,1,0:T(8,128)(2,1)S(1)} collective-permute-done((bf16[1,1536,128]{2,1,0:T(8,128)(2,1)S(1)}, bf16[1,1536,128]{2,1,0:T(8,128)(2,1)S(1)}, u32[]{:S(2)}, u32[]{:S(2)}) %collective-permute-start.12) | collective-permute-done | bytes 393248 | tf_op jit(solution)/shard_map/ppermute | solution.py:197
  170.3 0.0 collective-permute-done.6.refs_5_
  170.4 0.0 collective-permute-done.7.refs_6_
  170.4 0.7 copy-done.16
  171.1 0.3 copy-done.7
  171.4 0.9 copy-done.8
  172.3 0.0 collective-permute-done.8.refs_7_
  172.3 6.2 %shard_map.71 = f32[256,1536]{1,0:T(8,128)S(1)} custom-call(s32[3]{0:T(128)S(1)} %pad_add_fusion.core_ref.info_ref, bf16[16,520,128]{2,1,0:T(8,128)(2,1)S(1)} %all-to-all-done.arrived_ref, bf16[1,1536,128]{2,1,0:T(8,128)(2,1)} %refs_0_.3, bf16[1,1536,128]{2,1,0:T(8,128)(2,1)} %copy-done.10, bf16[1,1536,128]{2,1,0:T(8,128)(2,1)} %copy-done.11, ...), custom_call_target="tpu_custom_call" | custom-call | tf_op jit(solution)/shard_map/pallas_call | solution.py:237
  178.5 0.0 copy-start.1
  178.5 4.6 %collective-permute-start.13 = (f32[256,1536]{1,0:T(8,128)S(1)}, f32[256,1536]{1,0:T(8,128)S(1)}, u32[]{:S(2)}, u32[]{:S(2)}) collective-permute-start(f32[256,1536]{1,0:T(8,128)S(1)} %shard_map.71), channel_id=1, source_target_pairs={{1,0},{0,1},{3,2},{2,3},{5,4},{4,5},{7,6},{6,7},{9,8},{8,9},{11,10... | collective-permute-start | bytes 4718600 | tf_op jit(solution)/shard_map/ppermute | solution.py:248
  183.1 6.2 %shard_map.70.mine_ref = f32[256,1536]{1,0:T(8,128)S(1)} custom-call(s32[3]{0:T(128)S(1)} %pad_add_fusion.core_ref.info_ref, bf16[16,520,128]{2,1,0:T(8,128)(2,1)S(1)} %all-to-all-done.arrived_ref, bf16[1,1536,128]{2,1,0:T(8,128)(2,1)} %refs_0_.3, bf16[1,1536,128]{2,1,0:T(8,128)(2,1)} %copy-done.10, bf16[1,1536,128]{2,1,0:T(8,128)(2,1)} %copy-done.11, ...), custom_call_target="tpu_custom_call" | custom-call | tf_op jit(solution)/shard_map/pallas_call | solution.py:237
  189.3 0.0 collective-permute-done.13.theirs_ref
  189.3 0.0 copy-start.4
  189.3 3.0 %shard_map.72 = (bf16[256,3072]{1,0:T(8,128)(2,1)}, f32[16,8,128]{2,1,0:T(8,128)S(1)}) custom-call(s32[3]{0:T(128)S(1)} %pad_add_fusion.core_ref.info_ref, f32[256,1536]{1,0:T(8,128)S(1)} %shard_map.70.mine_ref, f32[256,1536]{1,0:T(8,128)S(1)} %collective-permute-done.13.theirs_ref, bf16[256,3072]{1,0:T(8,128)(2,1)S(1)} %bitcast.8, ...), custom_call_target="tpu_custom_call" | custom-call | tf_op jit(solution)/shard_map/pallas_call | solution.py:254
  192.3 21.7 %all_to_all.10.back_ref = f32[16,8,128]{2,1,0:T(8,128)S(1)} all-to-all(f32[16,8,128]{2,1,0:T(8,128)S(1)} %get-tuple-element.9), channel_id=1, replica_groups=mesh['zh'=2,'y'=8,'zl'=4,'x'=4,'c'=2] {'zh','y'}, dimensions={0} | all-to-all | bytes 131072 | tf_op jit(solution)/shard_map/all_to_all | solution.py:264
  214.1 0.8 shard_map.73
  (27 shorter events, 0.1 us)
Async XLA Ops:
  0.7 1.2 copy-start.2
  1.9 0.7 copy-start.3
  2.6 0.7 copy-start.5
  4.1 10.4 %collective-permute-start = (bf16[144,2048]{1,0:T(8,128)(2,1)S(1)}, bf16[144,2048]{1,0:T(8,128)(2,1)S(1)}, u32[]{:S(2)}, u32[]{:S(2)}) collective-permute-start(bf16[144,2048]{1,0:T(8,128)(2,1)S(1)} %get-tuple-element.7), channel_id=1, source_target_pairs={{1,0},{0,1},{3,2},{2,3},{5,4},{4,5},{7,6},{6,7},{9,8},{8,9},{11,10... | collective-permute-start | bytes 1769480 | tf_op jit(solution)/shard_map/ppermute | solution.py:227
  16.1 1.4 copy-start
  17.4 10.2 %copy-start.9 = (bf16[1,1536,128]{2,1,0:T(8,128)(2,1)S(1)}, bf16[1,1536,128]{2,1,0:T(8,128)(2,1)}, u32[]{:S(2)}) copy-start(bf16[1,1536,128]{2,1,0:T(8,128)(2,1)} %refs_0_.3) | copy-start | bytes 1179652
  17.4 154.9 %all-to-all-start = ((bf16[16,520,128]{2,1,0:T(8,128)(2,1)}), bf16[16,520,128]{2,1,0:T(8,128)(2,1)S(1)}, u32[]{:S(2)}, u32[]{:S(2)}) async-start(bf16[16,520,128]{2,1,0:T(8,128)(2,1)} %copy-done), calls=%async_computation | async-start | bytes 4259840 | tf_op jit(solution)/shard_map/all_to_all | solution.py:234
  27.6 59.3 %collective-permute-start.4 = (bf16[1,1536,128]{2,1,0:T(8,128)(2,1)S(1)}, bf16[1,1536,128]{2,1,0:T(8,128)(2,1)S(1)}, u32[]{:S(2)}, u32[]{:S(2)}) collective-permute-start(bf16[1,1536,128]{2,1,0:T(8,128)(2,1)S(1)} %copy-done.9), channel_id=1, source_target_pairs={{8,0},{16,8},{24,16},{0,24},{9,1},{17,9},{25,17},{1,25},{10,2},{18... | collective-permute-start | bytes 1179656 | tf_op jit(solution)/shard_map/ppermute | solution.py:197
  32.5 62.9 %collective-permute-start.5 = (bf16[1,1536,128]{2,1,0:T(8,128)(2,1)S(1)}, bf16[1,1536,128]{2,1,0:T(8,128)(2,1)S(1)}, u32[]{:S(2)}, u32[]{:S(2)}) collective-permute-start(bf16[1,1536,128]{2,1,0:T(8,128)(2,1)S(1)} %copy-done.9), channel_id=1, source_target_pairs={{24,0},{0,8},{8,16},{16,24},{25,1},{1,9},{9,17},{17,25},{26,2},{2,... | collective-permute-start | bytes 1179656 | tf_op jit(solution)/shard_map/ppermute | solution.py:197
  34.4 81.6 %collective-permute-start.1 = (bf16[1,1536,128]{2,1,0:T(8,128)(2,1)S(1)}, bf16[1,1536,128]{2,1,0:T(8,128)(2,1)S(1)}, u32[]{:S(2)}, u32[]{:S(2)}) collective-permute-start(bf16[1,1536,128]{2,1,0:T(8,128)(2,1)S(1)} %copy-done.9), channel_id=1, source_target_pairs={{2,0},{4,2},{6,4},{0,6},{3,1},{5,3},{7,5},{1,7},{10,8},{12,10},{14... | collective-permute-start | bytes 1179656 | tf_op jit(solution)/shard_map/ppermute | solution.py:197
  38.8 79.2 %collective-permute-start.2 = (bf16[1,1536,128]{2,1,0:T(8,128)(2,1)S(1)}, bf16[1,1536,128]{2,1,0:T(8,128)(2,1)S(1)}, u32[]{:S(2)}, u32[]{:S(2)}) collective-permute-start(bf16[1,1536,128]{2,1,0:T(8,128)(2,1)S(1)} %copy-done.9), channel_id=1, source_target_pairs={{6,0},{0,2},{2,4},{4,6},{7,1},{1,3},{3,5},{5,7},{14,8},{8,10},{10,... | collective-permute-start | bytes 1179656 | tf_op jit(solution)/shard_map/ppermute | solution.py:197
  40.8 80.9 %collective-permute-start.3 = (bf16[1,1536,128]{2,1,0:T(8,128)(2,1)S(1)}, bf16[1,1536,128]{2,1,0:T(8,128)(2,1)S(1)}, u32[]{:S(2)}, u32[]{:S(2)}) collective-permute-start(bf16[1,1536,128]{2,1,0:T(8,128)(2,1)S(1)} %copy-done.9), channel_id=1, source_target_pairs={{4,0},{6,2},{0,4},{2,6},{5,1},{7,3},{1,5},{3,7},{12,8},{14,10},{8,... | collective-permute-start | bytes 1179656 | tf_op jit(solution)/shard_map/ppermute | solution.py:197
  86.9 24.8 %collective-permute-start.9 = (bf16[1,1536,128]{2,1,0:T(8,128)(2,1)S(1)}, bf16[1,1536,128]{2,1,0:T(8,128)(2,1)S(1)}, u32[]{:S(2)}, u32[]{:S(2)}) collective-permute-start(bf16[1,1536,128]{2,1,0:T(8,128)(2,1)S(1)} %copy-done.9), channel_id=1, source_target_pairs={{16,0},{24,8},{0,16},{8,24},{17,1},{25,9},{1,17},{9,25},{18,2},{26... | collective-permute-start | bytes 1179656 | tf_op jit(solution)/shard_map/ppermute | solution.py:197
  95.5 76.8 %copy-start.6 = (bf16[2,1536,128]{2,1,0:T(8,128)(2,1)}, bf16[2,1536,128]{2,1,0:T(8,128)(2,1)S(1)}, u32[]{:S(2)}) copy-start(bf16[2,1536,128]{2,1,0:T(8,128)(2,1)S(1)} %constant_dynamic-update-slice_fusion.refs_4_) | copy-start | bytes 2359300
  95.5 74.8 %collective-permute-start.6 = (bf16[2,1536,128]{2,1,0:T(8,128)(2,1)S(1)}, bf16[2,1536,128]{2,1,0:T(8,128)(2,1)S(1)}, u32[]{:S(2)}, u32[]{:S(2)}) collective-permute-start(bf16[2,1536,128]{2,1,0:T(8,128)(2,1)S(1)} %constant_dynamic-update-slice_fusion.refs_4_), channel_id=1, source_target_pairs={{2,0},{4,2},{6,4},{0,6},{3,1},{5,3},{7,5},{1,7},{10,8},{12,10},{14... | collective-permute-start | bytes 2359304 | tf_op jit(solution)/shard_map/ppermute | solution.py:197
  111.7 58.7 %copy-start.13 = (bf16[1,1536,128]{2,1,0:T(8,128)(2,1)}, bf16[1,1536,128]{2,1,0:T(8,128)(2,1)S(1)}, u32[]{:S(2)}) copy-start(bf16[1,1536,128]{2,1,0:T(8,128)(2,1)S(1)} %collective-permute-done.9.refs_8_) | copy-start | bytes 1179652
  111.7 30.0 %collective-permute-start.10 = (bf16[1,1536,128]{2,1,0:T(8,128)(2,1)S(1)}, bf16[1,1536,128]{2,1,0:T(8,128)(2,1)S(1)}, u32[]{:S(2)}, u32[]{:S(2)}) collective-permute-start(bf16[1,1536,128]{2,1,0:T(8,128)(2,1)S(1)} %collective-permute-done.9.refs_8_), channel_id=1, source_target_pairs={{2,0},{4,2},{6,4},{0,6},{3,1},{5,3},{7,5},{1,7},{10,8},{12,10},{14... | collective-permute-start | bytes 1179656 | tf_op jit(solution)/shard_map/ppermute | solution.py:197
  116.1 54.3 %copy-start.10 = (bf16[1,1536,128]{2,1,0:T(8,128)(2,1)}, bf16[1,1536,128]{2,1,0:T(8,128)(2,1)S(1)}, u32[]{:S(2)}) copy-start(bf16[1,1536,128]{2,1,0:T(8,128)(2,1)S(1)} %collective-permute-done.1.refs_1_) | copy-start | bytes 1179652
  116.1 54.3 %collective-permute-start.7 = (bf16[2,1536,128]{2,1,0:T(8,128)(2,1)S(1)}, bf16[2,1536,128]{2,1,0:T(8,128)(2,1)S(1)}, u32[]{:S(2)}, u32[]{:S(2)}) collective-permute-start(bf16[2,1536,128]{2,1,0:T(8,128)(2,1)S(1)} %constant_dynamic-update-slice_fusion.refs_4_), channel_id=1, source_target_pairs={{6,0},{0,2},{2,4},{4,6},{7,1},{1,3},{3,5},{5,7},{14,8},{8,10},{10,... | collective-permute-start | bytes 2359304 | tf_op jit(solution)/shard_map/ppermute | solution.py:197
  118.0 52.4 %copy-start.11 = (bf16[1,1536,128]{2,1,0:T(8,128)(2,1)}, bf16[1,1536,128]{2,1,0:T(8,128)(2,1)S(1)}, u32[]{:S(2)}) copy-start(bf16[1,1536,128]{2,1,0:T(8,128)(2,1)S(1)} %collective-permute-done.2.refs_2_) | copy-start | bytes 1179652
  118.0 54.3 %collective-permute-start.8 = (bf16[2,1536,128]{2,1,0:T(8,128)(2,1)S(1)}, bf16[2,1536,128]{2,1,0:T(8,128)(2,1)}, u32[]{:S(2)}, u32[]{:S(2)}) collective-permute-start(bf16[2,1536,128]{2,1,0:T(8,128)(2,1)S(1)} %constant_dynamic-update-slice_fusion.refs_4_), channel_id=1, source_target_pairs={{4,0},{6,2},{0,4},{2,6},{5,1},{7,3},{1,5},{3,7},{12,8},{14,10},{8,... | collective-permute-start | bytes 2359304 | tf_op jit(solution)/shard_map/ppermute | solution.py:197
  121.7 48.7 %copy-start.12 = (bf16[1,1536,128]{2,1,0:T(8,128)(2,1)}, bf16[1,1536,128]{2,1,0:T(8,128)(2,1)S(1)}, u32[]{:S(2)}) copy-start(bf16[1,1536,128]{2,1,0:T(8,128)(2,1)S(1)} %collective-permute-done.3.refs_3_) | copy-start | bytes 1179652
  121.7 42.0 %collective-permute-start.11 = (bf16[1,1536,128]{2,1,0:T(8,128)(2,1)S(1)}, bf16[1,1536,128]{2,1,0:T(8,128)(2,1)S(1)}, u32[]{:S(2)}, u32[]{:S(2)}) collective-permute-start(bf16[1,1536,128]{2,1,0:T(8,128)(2,1)S(1)} %collective-permute-done.9.refs_8_), channel_id=1, source_target_pairs={{6,0},{0,2},{2,4},{4,6},{7,1},{1,3},{3,5},{5,7},{14,8},{8,10},{10,... | collective-permute-start | bytes 1179656 | tf_op jit(solution)/shard_map/ppermute | solution.py:197
  141.7 28.7 %copy-start.14 = (bf16[1,1536,128]{2,1,0:T(8,128)(2,1)}, bf16[1,1536,128]{2,1,0:T(8,128)(2,1)S(1)}, u32[]{:S(2)}) copy-start(bf16[1,1536,128]{2,1,0:T(8,128)(2,1)S(1)} %collective-permute-done.10.refs_9_) | copy-start | bytes 1179652
  141.7 28.7 %collective-permute-start.12 = (bf16[1,1536,128]{2,1,0:T(8,128)(2,1)S(1)}, bf16[1,1536,128]{2,1,0:T(8,128)(2,1)S(1)}, u32[]{:S(2)}, u32[]{:S(2)}) collective-permute-start(bf16[1,1536,128]{2,1,0:T(8,128)(2,1)S(1)} %collective-permute-done.9.refs_8_), channel_id=1, source_target_pairs={{4,0},{6,2},{0,4},{2,6},{5,1},{7,3},{1,5},{3,7},{12,8},{14,10},{8,... | collective-permute-start | bytes 1179656 | tf_op jit(solution)/shard_map/ppermute | solution.py:197
  163.7 8.6 %copy-start.15 = (bf16[1,1536,128]{2,1,0:T(8,128)(2,1)}, bf16[1,1536,128]{2,1,0:T(8,128)(2,1)S(1)}, u32[]{:S(2)}) copy-start(bf16[1,1536,128]{2,1,0:T(8,128)(2,1)S(1)} %collective-permute-done.11.refs_10_) | copy-start | bytes 1179652
  170.3 0.7 copy-start.16
  170.3 1.0 copy-start.7
  171.4 0.9 copy-start.8
  178.5 10.8 %copy-start.1 = (bf16[1,1,256,3072]{3,2,1,0:T(8,128)(2,1)S(1)}, bf16[1,1,256,3072]{3,2,1,0:T(8,128)(2,1)}, u32[]{:S(2)}) copy-start(bf16[1,1,256,3072]{3,2,1,0:T(8,128)(2,1)} %param.8) | copy-start | bytes 4718596
  178.5 10.8 %collective-permute-start.13 = (f32[256,1536]{1,0:T(8,128)S(1)}, f32[256,1536]{1,0:T(8,128)S(1)}, u32[]{:S(2)}, u32[]{:S(2)}) collective-permute-start(f32[256,1536]{1,0:T(8,128)S(1)} %shard_map.71), channel_id=1, source_target_pairs={{1,0},{0,1},{3,2},{2,3},{5,4},{4,5},{7,6},{6,7},{9,8},{8,9},{11,10... | collective-permute-start | bytes 4718600 | tf_op jit(solution)/shard_map/ppermute | solution.py:248
  189.3 24.8 %copy-start.4 = (s32[128,8]{0,1:T(8,128)S(1)}, s32[128,8]{0,1:T(8,128)}, u32[]{:S(2)}) copy-start(s32[128,8]{0,1:T(8,128)} %param.6) | copy-start | bytes 12292
where the time goes:
time: 216 us; the launch traced here: 215 us
  waiting for transfers between devices  106 us (49%)
  starting transfers between devices  61.9 us (29%)
  blocking collectives  21.7 us (10%)
  Pallas kernels  18.6 us (9%)
  local copies, waits for them, and re-layouts  5.94 us (3%)
    ppermute x12, waiting for transfers between devices, permute(): return lax.ppermute(array, axis, ring(4, shift))  104 us
    ppermute x12, starting transfers between devices, permute(): return lax.ppermute(array, axis, ring(4, shift))  38.4 us
    all_to_all x1, blocking collectives, step(): back = lax.all_to_all(score, EP, split_axis=0, concat_axis=0, tiled=True)  21.7 us
    pallas_call x2, Pallas kernels, step(): call(functools.partial(matmul_kernel, shifts, other), jax.ShapeDtypeStruc...  12.4 us
    all_to_all x1, starting transfers between devices, step(): lax.all_to_all(outgoing, EP, split_axis=0, concat_axis=0, tiled=True)  10.2 us
    ppermute x1, starting transfers between devices, step(): got = lax.ppermute(send, 'c', ring(2, 1))  8.75 us
    unnamed x35, local copies, waits for them, and re-layouts  5.88 us
    ppermute x1, starting transfers between devices, step(): theirs = lax.ppermute(theirs, 'c', ring(2, 1))  4.56 us
  transfers between devices with their start and end apart: 15, of which 7 were waited for; matrix products, arithmetic and copies ran while one was open for 0% of the time, Pallas kernels for 3%

commit v1 on v0

--- a/solution.py
+++ b/solution.py
@@ -111,8 +111,9 @@
     ).astype(BF16)
 
 
-def matmul_kernel(shifts, other, info_ref, arrived_ref, *refs):
-    weights, (out_ref, rows_ref) = refs[:-2], refs[-2:]
+def matmul_kernel(shifts, other, more, info_ref, arrived_ref, *refs):
+    refs, (out_ref, rows_ref) = refs[:-2], refs[-2:]
+    weights = refs[1:] if more else refs
     parts = [(w, i) for w in weights for i in range(w.shape[0])]
 
     @pl.when(pl.program_id(0) == 0)
@@ -128,9 +129,10 @@
             ].reshape(slots, LANES)
 
     block = jnp.concatenate([w[i] for w, i in parts], axis=1)
-    out_ref[...] = lax.dot_general(
+    out = lax.dot_general(
         rows_ref[...], block, (((1,), (1,)), ((), ())), preferred_element_type=F32
     )
+    out_ref[...] = refs[0][...] + out if more else out
 
 
 def finish_kernel(info_ref, mine_ref, theirs_ref, saved_ref, gate_ref, out_ref, score_ref):
@@ -199,30 +201,30 @@
 
 def gather_weights(block):
     z1, z3, z2 = (permute(block, "zl", r) for r in (1, 3, 2))
-    first = [block] + [permute(block, "x", r) for r in (1, 3, 2)]
-    pair = jnp.concatenate([z1, z3], axis=0)
-    second = [pair] + [permute(pair, "x", r) for r in (1, 3, 2)]
-    third = [z2] + [permute(z2, "x", r) for r in (1, 3, 2)]
-    groups, shifts = [], []
-    for arrays, zs in ((first, (0,)), (second, (1, 3)), (third, (2,))):
-        for array, r in zip(arrays, (0, 1, 3, 2)):
-            groups.append(array)
-            shifts += [(dz, r) for dz in zs]
-    return groups, shifts
+    trio = jnp.concatenate([block, z1, z3], axis=0)
+    up, down = permute(trio, "x", 1), permute(trio, "x", 3)
+    up2, down2 = permute(z2, "x", 1), permute(z2, "x", 3)
+    far1 = permute(up[:2], "x", 1)
+    far3 = permute(down[2:], "x", 3)
+    last = permute(down2, "x", 3)
+    early = [(trio, (0, 1, 3), 0), (z2, (2,), 0), (up, (0, 1, 3), 1)]
+    early += [(down, (0, 1, 3), 3), (up2, (2,), 1), (down2, (2,), 3)]
+    late = [(far1, (0, 1), 2), (far3, (3,), 2), (last, (2,), 2)]
+    return early, late
 
 
 def step(grad_out, routes, gate, saved, w_down):
     tokens, width = grad_out.shape
     units, slots = w_down.shape[1], saved.shape[2]
     sources = slots // CAPACITY
-    groups, shifts = gather_weights(w_down)
+    early, late = gather_weights(w_down)
     info = jnp.stack([lax.axis_index(a) for a in ("c", "zl", "x")]).astype(jnp.int32)
     half = width // 2
     blocks = half // LANES
     routes_t, gate_t = routes.T, gate.T
     packed = jax.ShapeDtypeStruct((tokens + 16, half), BF16)
     keep, send = call(pack_kernel, (packed, packed), [SMEM, VMEM, VMEM, VMEM], (VMEM, VMEM))(
-        info, grad_out, routes_t, gate_t
+        info, far(grad_out), far(routes_t), far(gate_t)
     )
     got = lax.ppermute(send, "c", ring(2, 1))
     outgoing = call(
@@ -233,18 +235,24 @@
     )(info, keep, got)
     arrived = lax.all_to_all(outgoing, EP, split_axis=0, concat_axis=0, tiled=True)
     part = 256
-    theirs, mine = (
-        call(
-            functools.partial(matmul_kernel, shifts, other),
+    piece = pl.BlockSpec((slots, part), lambda j: (0, j))
+
+    def product(groups, other, *more):
+        shifts = [(dz, dx) for _, dzs, dx in groups for dz in dzs]
+        arrays = [a for a, _, _ in groups]
+        return call(
+            functools.partial(matmul_kernel, shifts, other, bool(more)),
             jax.ShapeDtypeStruct((slots, units), F32),
             [SMEM, VMEM]
-            + [pl.BlockSpec((g.shape[0], part, LANES), lambda j: (0, j, 0)) for g in groups],
-            pl.BlockSpec((slots, part), lambda j: (0, j)),
-            [pltpu.VMEM((slots, half), BF16)],
+            + [piece] * len(more)
+            + [pl.BlockSpec((a.shape[0], part, LANES), lambda j: (0, j, 0)) for a in arrays],
+            piece,
+            [pltpu.VMEM((slots, len(shifts) * LANES), BF16)],
             (units // part,),
-        )(info, near(arrived), *map(far, groups))
-        for other in (True, False)
-    )
+        )(info, near(arrived), *more, *map(far, arrays))
+
+    theirs = product(late, True, product(early, True))
+    mine = product(early + late, False)
     theirs = lax.ppermute(theirs, "c", ring(2, 1))
     gates = arrived[:, 2 * CAPACITY * blocks :, :]
     steps = 4

time: 216 us -> 205 us (0.949)
  starting transfers between devices: 61.9 us -> 52 us
  waiting for transfers between devices: 106 us -> 98.3 us
  Pallas kernels: 18.6 us -> 22.9 us
  blocking collectives: 21.7 us -> 25.3 us
  local copies, waits for them, and re-layouts: 5.94 us -> 3.4 us
    ppermute x12 -> x10, starting transfers between devices: 38.4 us -> 28.7 us  [permute(): return lax.ppermute(array, axis, ring(4, shift))]
    ppermute x12 -> x10, waiting for transfers between devices: 104 us -> 96.7 us  [permute(): return lax.ppermute(array, axis, ring(4, shift))]
    unnamed x35 -> x20, local copies, waits for them, and re-layouts: 5.88 us -> 1.45 us
    pallas_call x2 -> x3, Pallas kernels: 12.4 us -> 16 us  [product(): call(functools.partial(matmul_kernel, shifts, other, bool(more)), jax.Sha...]
    all_to_all x1, blocking collectives: 21.7 us -> 25.3 us  [step(): back = lax.all_to_all(score, EP, split_axis=0, concat_axis=0, tiled=True)]
  transfers between devices with their start and end apart: 15 -> 13, of which waited for: 7 -> 6; matrix products, arithmetic and copies ran while one was open for 0% -> 1% of each run, Pallas kernels for 3% -> 6%
where the time goes in v1:
time: 205 us; the launch traced here: 203 us
  waiting for transfers between devices  98.3 us (48%)
  starting transfers between devices  52 us (25%)
  blocking collectives  25.3 us (12%)
  Pallas kernels  22.9 us (11%)
  local copies, waits for them, and re-layouts  3.4 us (2%)
    ppermute x10, waiting for transfers between devices, permute(): return lax.ppermute(array, axis, ring(4, shift))  96.7 us
    ppermute x10, starting transfers between devices, permute(): return lax.ppermute(array, axis, ring(4, shift))  28.7 us
    all_to_all x1, blocking collectives, step(): back = lax.all_to_all(score, EP, split_axis=0, concat_axis=0, tiled=True)  25.3 us
    pallas_call x3, Pallas kernels, product(): call(functools.partial(matmul_kernel, shifts, other, bool(more)), jax.Sha...  16 us
    all_to_all x1, starting transfers between devices, step(): lax.all_to_all(outgoing, EP, split_axis=0, concat_axis=0, tiled=True)  10.2 us
    ppermute x1, starting transfers between devices, step(): got = lax.ppermute(send, 'c', ring(2, 1))  8.74 us
    ppermute x1, starting transfers between devices, step(): theirs = lax.ppermute(theirs, 'c', ring(2, 1))  4.42 us
  transfers between devices with their start and end apart: 13, of which 6 were waited for; matrix products, arithmetic and copies ran while one was open for 1% of the time, Pallas kernels for 6%

profile of v1, /device:TPU:1, one launch (start us, length us, event | category | flops | bytes accessed | tf_op | source)
XLA Modules:
  0.0 203.0 jit_solution(16986256651846912605)
XLA Ops:
  0.6 0.1 pad_add_fusion.core_ref.info_ref
  0.7 1.5 shard_map.68
  2.3 8.7 %collective-permute-start = (bf16[144,2048]{1,0:T(8,128)(2,1)S(1)}, bf16[144,2048]{1,0:T(8,128)(2,1)S(1)}, u32[]{:S(2)}, u32[]{:S(2)}) collective-permute-start(bf16[144,2048]{1,0:T(8,128)(2,1)S(1)} %get-tuple-element.7), channel_id=1, source_target_pairs={{1,0},{0,1},{3,2},{2,3},{5,4},{4,5},{7,6},{6,7},{9,8},{8,9},{11,10... | collective-permute-start | bytes 1769480 | tf_op jit(solution)/shard_map/ppermute | solution.py:229
  11.0 1.6 collective-permute-done.got_ref
  12.6 1.6 shard_map.69
  14.2 0.0 copy-start
  14.2 1.3 copy-done
  15.5 10.2 %all-to-all-start = ((bf16[16,520,128]{2,1,0:T(8,128)(2,1)}), bf16[16,520,128]{2,1,0:T(8,128)(2,1)S(1)}, u32[]{:S(2)}, u32[]{:S(2)}) async-start(bf16[16,520,128]{2,1,0:T(8,128)(2,1)} %copy-done), calls=%async_computation | async-start | bytes 4259840 | tf_op jit(solution)/shard_map/all_to_all | solution.py:236
  25.7 0.0 copy-done.7
  25.7 0.0 copy-start.8
  25.7 5.1 %collective-permute-start.1 = (bf16[1,1536,128]{2,1,0:T(8,128)(2,1)S(1)}, bf16[1,1536,128]{2,1,0:T(8,128)(2,1)S(1)}, u32[]{:S(2)}, u32[]{:S(2)}) collective-permute-start(bf16[1,1536,128]{2,1,0:T(8,128)(2,1)S(1)} %copy-done.7), channel_id=1, source_target_pairs={{8,0},{16,8},{24,16},{0,24},{9,1},{17,9},{25,17},{1,25},{10,2},{18... | collective-permute-start | bytes 1179656 | tf_op jit(solution)/shard_map/ppermute | solution.py:199
  30.8 1.9 collective-permute-start.2
  32.7 52.0 %collective-permute-done.1 = bf16[1,1536,128]{2,1,0:T(8,128)(2,1)S(1)} collective-permute-done((bf16[1,1536,128]{2,1,0:T(8,128)(2,1)S(1)}, bf16[1,1536,128]{2,1,0:T(8,128)(2,1)S(1)}, u32[]{:S(2)}, u32[]{:S(2)}) %collective-permute-start.1) | collective-permute-done | bytes 393248 | tf_op jit(solution)/shard_map/ppermute | solution.py:199
  84.7 0.1 constant_dynamic-update-slice_fusion.1
  84.8 9.0 %collective-permute-done.2 = bf16[1,1536,128]{2,1,0:T(8,128)(2,1)S(1)} collective-permute-done((bf16[1,1536,128]{2,1,0:T(8,128)(2,1)S(1)}, bf16[1,1536,128]{2,1,0:T(8,128)(2,1)S(1)}, u32[]{:S(2)}, u32[]{:S(2)}) %collective-permute-start.2) | collective-permute-done | bytes 393248 | tf_op jit(solution)/shard_map/ppermute | solution.py:199
  93.8 0.1 constant_dynamic-update-slice_fusion.refs_0_
  93.8 0.0 copy-start.5
  93.8 4.5 %collective-permute-start.4 = (bf16[3,1536,128]{2,1,0:T(8,128)(2,1)S(1)}, bf16[3,1536,128]{2,1,0:T(8,128)(2,1)S(1)}, u32[]{:S(2)}, u32[]{:S(2)}) collective-permute-start(bf16[3,1536,128]{2,1,0:T(8,128)(2,1)S(1)} %constant_dynamic-update-slice_fusion.refs_0_), channel_id=1, source_target_pairs={{2,0},{4,2},{6,4},{0,6},{3,1},{5,3},{7,5},{1,7},{10,8},{12,10},{14... | collective-permute-start | bytes 3538952 | tf_op jit(solution)/shard_map/ppermute | solution.py:199
  98.4 1.9 collective-permute-start.5
  100.3 0.0 copy-done.8
  100.3 1.9 collective-permute-start.3
  102.2 19.0 %collective-permute-done.3.refs_1_ = bf16[1,1536,128]{2,1,0:T(8,128)(2,1)S(1)} collective-permute-done((bf16[1,1536,128]{2,1,0:T(8,128)(2,1)S(1)}, bf16[1,1536,128]{2,1,0:T(8,128)(2,1)S(1)}, u32[]{:S(2)}, u32[]{:S(2)}) %collective-permute-start.3) | collective-permute-done | bytes 393248 | tf_op jit(solution)/shard_map/ppermute | solution.py:199
  121.2 1.9 collective-permute-start.7
  123.2 0.0 collective-permute-done.4.refs_2_
  123.2 1.0 slice.12
  124.2 5.1 %collective-permute-start.8 = (bf16[2,1536,128]{2,1,0:T(8,128)(2,1)}, bf16[2,1536,128]{2,1,0:T(8,128)(2,1)}, u32[]{:S(2)}, u32[]{:S(2)}) collective-permute-start(bf16[2,1536,128]{2,1,0:T(8,128)(2,1)} %slice.12), channel_id=1, source_target_pairs={{2,0},{4,2},{6,4},{0,6},{3,1},{5,3},{7,5},{1,7},{10,8},{12,10},{14... | collective-permute-start | bytes 2359304 | tf_op jit(solution)/shard_map/ppermute | solution.py:199
  129.3 2.5 %collective-permute-start.6 = (bf16[1,1536,128]{2,1,0:T(8,128)(2,1)S(1)}, bf16[1,1536,128]{2,1,0:T(8,128)(2,1)}, u32[]{:S(2)}, u32[]{:S(2)}) collective-permute-start(bf16[1,1536,128]{2,1,0:T(8,128)(2,1)S(1)} %collective-permute-done.3.refs_1_), channel_id=1, source_target_pairs={{2,0},{4,2},{6,4},{0,6},{3,1},{5,3},{7,5},{1,7},{10,8},{12,10},{14... | collective-permute-start | bytes 1179656 | tf_op jit(solution)/shard_map/ppermute | solution.py:199
  131.8 4.7 %collective-permute-done.7.refs_5_ = bf16[1,1536,128]{2,1,0:T(8,128)(2,1)} collective-permute-done((bf16[1,1536,128]{2,1,0:T(8,128)(2,1)S(1)}, bf16[1,1536,128]{2,1,0:T(8,128)(2,1)}, u32[]{:S(2)}, u32[]{:S(2)}) %collective-permute-start.7) | collective-permute-done | bytes 393248 | tf_op jit(solution)/shard_map/ppermute | solution.py:199
  136.6 1.9 collective-permute-start.10
  138.5 0.0 collective-permute-done.5.refs_3_
  138.5 0.9 slice.13
  139.4 1.9 collective-permute-start.9
  141.3 12.0 %collective-permute-done.6.refs_4_ = bf16[1,1536,128]{2,1,0:T(8,128)(2,1)} collective-permute-done((bf16[1,1536,128]{2,1,0:T(8,128)(2,1)S(1)}, bf16[1,1536,128]{2,1,0:T(8,128)(2,1)}, u32[]{:S(2)}, u32[]{:S(2)}) %collective-permute-start.6) | collective-permute-done | bytes 393248 | tf_op jit(solution)/shard_map/ppermute | solution.py:199
  153.3 0.0 all-to-all-done.arrived_ref
  153.3 5.5 %shard_map.71.refs_0_ = f32[256,1536]{1,0:T(8,128)S(1)} custom-call(s32[3]{0:T(128)S(1)} %pad_add_fusion.core_ref.info_ref, bf16[16,520,128]{2,1,0:T(8,128)(2,1)S(1)} %all-to-all-done.arrived_ref, bf16[3,1536,128]{2,1,0:T(8,128)(2,1)} %copy-done.5, bf16[1,1536,128]{2,1,0:T(8,128)(2,1)} %copy-done.6, bf16[3,1536,128]{2,1,0:T(8,128)(2,1)} %copy-done.3, ...), custom_call_target="tpu_custom_call" | custom-call | tf_op jit(solution)/shard_map/pallas_call | solution.py:243
  158.8 0.0 collective-permute-done.10.refs_8_.refs_3_
  158.8 0.0 collective-permute-done.9.refs_7_.refs_2_
  158.8 0.0 collective-permute-done.8.refs_6_.refs_1_
  158.8 4.2 %shard_map.72 = f32[256,1536]{1,0:T(8,128)S(1)} custom-call(s32[3]{0:T(128)S(1)} %pad_add_fusion.core_ref.info_ref, bf16[16,520,128]{2,1,0:T(8,128)(2,1)S(1)} %all-to-all-done.arrived_ref, f32[256,1536]{1,0:T(8,128)S(1)} %shard_map.71.refs_0_, bf16[2,1536,128]{2,1,0:T(8,128)(2,1)} %collective-permute-done.8.refs_6_.refs_1_, ...), custom_call_target="tpu_custom_call" | custom-call | tf_op jit(solution)/shard_map/pallas_call | solution.py:243
  163.1 0.0 copy-start.1
  163.1 4.4 %collective-permute-start.11 = (f32[256,1536]{1,0:T(8,128)S(1)}, f32[256,1536]{1,0:T(8,128)S(1)}, u32[]{:S(2)}, u32[]{:S(2)}) collective-permute-start(f32[256,1536]{1,0:T(8,128)S(1)} %shard_map.72), channel_id=1, source_target_pairs={{1,0},{0,1},{3,2},{2,3},{5,4},{4,5},{7,6},{6,7},{9,8},{8,9},{11,10... | collective-permute-start | bytes 4718600 | tf_op jit(solution)/shard_map/ppermute | solution.py:256
  167.5 6.3 %shard_map.70.mine_ref = f32[256,1536]{1,0:T(8,128)S(1)} custom-call(s32[3]{0:T(128)S(1)} %pad_add_fusion.core_ref.info_ref, bf16[16,520,128]{2,1,0:T(8,128)(2,1)S(1)} %all-to-all-done.arrived_ref, bf16[3,1536,128]{2,1,0:T(8,128)(2,1)} %copy-done.5, bf16[1,1536,128]{2,1,0:T(8,128)(2,1)} %copy-done.6, bf16[3,1536,128]{2,1,0:T(8,128)(2,1)} %copy-done.3, ...), custom_call_target="tpu_custom_call" | custom-call | tf_op jit(solution)/shard_map/pallas_call | solution.py:243
  173.8 0.0 collective-permute-done.11.theirs_ref
  173.8 0.0 copy-done.1
  173.8 0.0 copy-start.2
  173.8 3.0 %shard_map.73 = (bf16[256,3072]{1,0:T(8,128)(2,1)}, f32[16,8,128]{2,1,0:T(8,128)S(1)}) custom-call(s32[3]{0:T(128)S(1)} %pad_add_fusion.core_ref.info_ref, f32[256,1536]{1,0:T(8,128)S(1)} %shard_map.70.mine_ref, f32[256,1536]{1,0:T(8,128)S(1)} %collective-permute-done.11.theirs_ref, bf16[256,3072]{1,0:T(8,128)(2,1)S(1)} %bitcast.8, ...), custom_call_target="tpu_custom_call" | custom-call | tf_op jit(solution)/shard_map/pallas_call | solution.py:262
  176.9 25.3 %all_to_all.10.back_ref = f32[16,8,128]{2,1,0:T(8,128)S(1)} all-to-all(f32[16,8,128]{2,1,0:T(8,128)S(1)} %get-tuple-element.9), channel_id=1, replica_groups=mesh['zh'=2,'y'=8,'zl'=4,'x'=4,'c'=2] {'zh','y'}, dimensions={0} | all-to-all | bytes 131072 | tf_op jit(solution)/shard_map/all_to_all | solution.py:272
  202.2 0.8 shard_map.74
  (11 shorter events, 0.0 us)
Async XLA Ops:
  2.3 10.4 %collective-permute-start = (bf16[144,2048]{1,0:T(8,128)(2,1)S(1)}, bf16[144,2048]{1,0:T(8,128)(2,1)S(1)}, u32[]{:S(2)}, u32[]{:S(2)}) collective-permute-start(bf16[144,2048]{1,0:T(8,128)(2,1)S(1)} %get-tuple-element.7), channel_id=1, source_target_pairs={{1,0},{0,1},{3,2},{2,3},{5,4},{4,5},{7,6},{6,7},{9,8},{8,9},{11,10... | collective-permute-start | bytes 1769480 | tf_op jit(solution)/shard_map/ppermute | solution.py:229
  14.2 1.3 copy-start
  15.5 10.2 %copy-start.7 = (bf16[1,1536,128]{2,1,0:T(8,128)(2,1)S(1)}, bf16[1,1536,128]{2,1,0:T(8,128)(2,1)}, u32[]{:S(2)}) copy-start(bf16[1,1536,128]{2,1,0:T(8,128)(2,1)} %param.9) | copy-start | bytes 1179652
  15.5 137.8 %all-to-all-start = ((bf16[16,520,128]{2,1,0:T(8,128)(2,1)}), bf16[16,520,128]{2,1,0:T(8,128)(2,1)S(1)}, u32[]{:S(2)}, u32[]{:S(2)}) async-start(bf16[16,520,128]{2,1,0:T(8,128)(2,1)} %copy-done), calls=%async_computation | async-start | bytes 4259840 | tf_op jit(solution)/shard_map/all_to_all | solution.py:236
  25.7 74.6 %copy-start.8 = (bf16[1,1536,128]{2,1,0:T(8,128)(2,1)S(1)}, bf16[1,1536,128]{2,1,0:T(8,128)(2,1)}, u32[]{:S(2)}) copy-start(bf16[1,1536,128]{2,1,0:T(8,128)(2,1)} %param.9) | copy-start | bytes 1179652
  25.7 59.0 %collective-permute-start.1 = (bf16[1,1536,128]{2,1,0:T(8,128)(2,1)S(1)}, bf16[1,1536,128]{2,1,0:T(8,128)(2,1)S(1)}, u32[]{:S(2)}, u32[]{:S(2)}) collective-permute-start(bf16[1,1536,128]{2,1,0:T(8,128)(2,1)S(1)} %copy-done.7), channel_id=1, source_target_pairs={{8,0},{16,8},{24,16},{0,24},{9,1},{17,9},{25,17},{1,25},{10,2},{18... | collective-permute-start | bytes 1179656 | tf_op jit(solution)/shard_map/ppermute | solution.py:199
  30.8 63.0 %collective-permute-start.2 = (bf16[1,1536,128]{2,1,0:T(8,128)(2,1)S(1)}, bf16[1,1536,128]{2,1,0:T(8,128)(2,1)S(1)}, u32[]{:S(2)}, u32[]{:S(2)}) collective-permute-start(bf16[1,1536,128]{2,1,0:T(8,128)(2,1)S(1)} %copy-done.7), channel_id=1, source_target_pairs={{24,0},{0,8},{8,16},{16,24},{25,1},{1,9},{9,17},{17,25},{26,2},{2,... | collective-permute-start | bytes 1179656 | tf_op jit(solution)/shard_map/ppermute | solution.py:199
  93.8 47.5 %copy-start.5 = (bf16[3,1536,128]{2,1,0:T(8,128)(2,1)}, bf16[3,1536,128]{2,1,0:T(8,128)(2,1)S(1)}, u32[]{:S(2)}) copy-start(bf16[3,1536,128]{2,1,0:T(8,128)(2,1)S(1)} %constant_dynamic-update-slice_fusion.refs_0_) | copy-start | bytes 3538948
  93.8 29.3 %collective-permute-start.4 = (bf16[3,1536,128]{2,1,0:T(8,128)(2,1)S(1)}, bf16[3,1536,128]{2,1,0:T(8,128)(2,1)S(1)}, u32[]{:S(2)}, u32[]{:S(2)}) collective-permute-start(bf16[3,1536,128]{2,1,0:T(8,128)(2,1)S(1)} %constant_dynamic-update-slice_fusion.refs_0_), channel_id=1, source_target_pairs={{2,0},{4,2},{6,4},{0,6},{3,1},{5,3},{7,5},{1,7},{10,8},{12,10},{14... | collective-permute-start | bytes 3538952 | tf_op jit(solution)/shard_map/ppermute | solution.py:199
  98.4 40.1 %collective-permute-start.5 = (bf16[3,1536,128]{2,1,0:T(8,128)(2,1)S(1)}, bf16[3,1536,128]{2,1,0:T(8,128)(2,1)S(1)}, u32[]{:S(2)}, u32[]{:S(2)}) collective-permute-start(bf16[3,1536,128]{2,1,0:T(8,128)(2,1)S(1)} %constant_dynamic-update-slice_fusion.refs_0_), channel_id=1, source_target_pairs={{6,0},{0,2},{2,4},{4,6},{7,1},{1,3},{3,5},{5,7},{14,8},{8,10},{10,... | collective-permute-start | bytes 3538952 | tf_op jit(solution)/shard_map/ppermute | solution.py:199
  100.3 20.9 %collective-permute-start.3 = (bf16[1,1536,128]{2,1,0:T(8,128)(2,1)S(1)}, bf16[1,1536,128]{2,1,0:T(8,128)(2,1)S(1)}, u32[]{:S(2)}, u32[]{:S(2)}) collective-permute-start(bf16[1,1536,128]{2,1,0:T(8,128)(2,1)S(1)} %copy-done.8), channel_id=1, source_target_pairs={{16,0},{24,8},{0,16},{8,24},{17,1},{25,9},{1,17},{9,25},{18,2},{26... | collective-permute-start | bytes 1179656 | tf_op jit(solution)/shard_map/ppermute | solution.py:199
  121.2 20.1 %copy-start.6 = (bf16[1,1536,128]{2,1,0:T(8,128)(2,1)}, bf16[1,1536,128]{2,1,0:T(8,128)(2,1)S(1)}, u32[]{:S(2)}) copy-start(bf16[1,1536,128]{2,1,0:T(8,128)(2,1)S(1)} %collective-permute-done.3.refs_1_) | copy-start | bytes 1179652
  121.2 15.3 %collective-permute-start.7 = (bf16[1,1536,128]{2,1,0:T(8,128)(2,1)S(1)}, bf16[1,1536,128]{2,1,0:T(8,128)(2,1)}, u32[]{:S(2)}, u32[]{:S(2)}) collective-permute-start(bf16[1,1536,128]{2,1,0:T(8,128)(2,1)S(1)} %collective-permute-done.3.refs_1_), channel_id=1, source_target_pairs={{6,0},{0,2},{2,4},{4,6},{7,1},{1,3},{3,5},{5,7},{14,8},{8,10},{10,... | collective-permute-start | bytes 1179656 | tf_op jit(solution)/shard_map/ppermute | solution.py:199
  123.2 30.2 %copy-start.3 = (bf16[3,1536,128]{2,1,0:T(8,128)(2,1)}, bf16[3,1536,128]{2,1,0:T(8,128)(2,1)S(1)}, u32[]{:S(2)}) copy-start(bf16[3,1536,128]{2,1,0:T(8,128)(2,1)S(1)} %collective-permute-done.4.refs_2_) | copy-start | bytes 3538948
  124.2 34.6 %collective-permute-start.8 = (bf16[2,1536,128]{2,1,0:T(8,128)(2,1)}, bf16[2,1536,128]{2,1,0:T(8,128)(2,1)}, u32[]{:S(2)}, u32[]{:S(2)}) collective-permute-start(bf16[2,1536,128]{2,1,0:T(8,128)(2,1)} %slice.12), channel_id=1, source_target_pairs={{2,0},{4,2},{6,4},{0,6},{3,1},{5,3},{7,5},{1,7},{10,8},{12,10},{14... | collective-permute-start | bytes 2359304 | tf_op jit(solution)/shard_map/ppermute | solution.py:199
  129.3 24.0 %collective-permute-start.6 = (bf16[1,1536,128]{2,1,0:T(8,128)(2,1)S(1)}, bf16[1,1536,128]{2,1,0:T(8,128)(2,1)}, u32[]{:S(2)}, u32[]{:S(2)}) collective-permute-start(bf16[1,1536,128]{2,1,0:T(8,128)(2,1)S(1)} %collective-permute-done.3.refs_1_), channel_id=1, source_target_pairs={{2,0},{4,2},{6,4},{0,6},{3,1},{5,3},{7,5},{1,7},{10,8},{12,10},{14... | collective-permute-start | bytes 1179656 | tf_op jit(solution)/shard_map/ppermute | solution.py:199
  136.6 22.2 %collective-permute-start.10 = (bf16[1,1536,128]{2,1,0:T(8,128)(2,1)}, bf16[1,1536,128]{2,1,0:T(8,128)(2,1)}, u32[]{:S(2)}, u32[]{:S(2)}) collective-permute-start(bf16[1,1536,128]{2,1,0:T(8,128)(2,1)} %collective-permute-done.7.refs_5_), channel_id=1, source_target_pairs={{6,0},{0,2},{2,4},{4,6},{7,1},{1,3},{3,5},{5,7},{14,8},{8,10},{10,... | collective-permute-start | bytes 1179656 | tf_op jit(solution)/shard_map/ppermute | solution.py:199
  138.5 2.8 %copy-start.4 = (bf16[3,1536,128]{2,1,0:T(8,128)(2,1)}, bf16[3,1536,128]{2,1,0:T(8,128)(2,1)S(1)}, u32[]{:S(2)}) copy-start(bf16[3,1536,128]{2,1,0:T(8,128)(2,1)S(1)} %collective-permute-done.5.refs_3_) | copy-start | bytes 3538948
  139.4 19.4 %collective-permute-start.9 = (bf16[1,1536,128]{2,1,0:T(8,128)(2,1)}, bf16[1,1536,128]{2,1,0:T(8,128)(2,1)}, u32[]{:S(2)}, u32[]{:S(2)}) collective-permute-start(bf16[1,1536,128]{2,1,0:T(8,128)(2,1)} %slice.13), channel_id=1, source_target_pairs={{6,0},{0,2},{2,4},{4,6},{7,1},{1,3},{3,5},{5,7},{14,8},{8,10},{10,... | collective-permute-start | bytes 1179656 | tf_op jit(solution)/shard_map/ppermute | solution.py:199
  163.1 10.7 %copy-start.1 = (bf16[1,1,256,3072]{3,2,1,0:T(8,128)(2,1)S(1)}, bf16[1,1,256,3072]{3,2,1,0:T(8,128)(2,1)}, u32[]{:S(2)}) copy-start(bf16[1,1,256,3072]{3,2,1,0:T(8,128)(2,1)} %param.8) | copy-start | bytes 4718596
  163.1 10.7 %collective-permute-start.11 = (f32[256,1536]{1,0:T(8,128)S(1)}, f32[256,1536]{1,0:T(8,128)S(1)}, u32[]{:S(2)}, u32[]{:S(2)}) collective-permute-start(f32[256,1536]{1,0:T(8,128)S(1)} %shard_map.72), channel_id=1, source_target_pairs={{1,0},{0,1},{3,2},{2,3},{5,4},{4,5},{7,6},{6,7},{9,8},{8,9},{11,10... | collective-permute-start | bytes 4718600 | tf_op jit(solution)/shard_map/ppermute | solution.py:256
  173.8 28.4 %copy-start.2 = (s32[128,8]{0,1:T(8,128)S(1)}, s32[128,8]{0,1:T(8,128)}, u32[]{:S(2)}) copy-start(s32[128,8]{0,1:T(8,128)} %param.6) | copy-start | bytes 12292

commit v2 on v0

v2 whole, which is shorter than its diff:
```python
import functools

import jax
import jax.numpy as jnp
from jax import lax
from jax.experimental import pallas as pl
from jax.experimental.pallas import tpu as pltpu
from jax.sharding import Mesh, PartitionSpec as P


LANES = 128
CAPACITY = 16
STEP = 8
EP = ("zh", "y")
F32, BF16 = jnp.float32, jnp.bfloat16
VMEM = pl.BlockSpec(memory_space=pltpu.VMEM)
SMEM = pl.BlockSpec(memory_space=pltpu.SMEM)


def ring(size, shift):
    return [((i + shift) % size, i) for i in range(size)]


def pack_kernel(core_ref, tokens_ref, routes_ref, keep_ref, send_ref):
    core = core_ref[0]
    rows = tokens_ref.shape[0]
    for ref, parity in ((keep_ref, core), (send_ref, 1 - core)):
        for b in range(ref.shape[1] // LANES):
            start = pl.multiple_of((2 * b + parity) * LANES, LANES)
            ref[:rows, b * LANES : (b + 1) * LANES] = tokens_ref[:, pl.ds(start, LANES)]
    send_ref[rows:, :] = jnp.zeros((send_ref.shape[0] - rows, send_ref.shape[1]), BF16)
    routes = routes_ref[...].astype(F32)
    send_ref[rows:, :LANES] = jnp.concatenate([routes, routes], axis=0).astype(BF16)


def places(routes, experts):
    tokens = routes.shape[1]
    wanted = (STEP * lax.broadcasted_iota(jnp.int32, (experts, tokens), 0)).astype(F32)
    hits = [routes[k : k + 1, :] == wanted for k in range(routes.shape[0])]
    member = functools.reduce(jnp.add, [h.astype(F32) for h in hits])
    before = lax.broadcasted_iota(jnp.int32, (tokens, tokens), 0) < lax.broadcasted_iota(
        jnp.int32, (tokens, tokens), 1
    )
    place = lax.dot_general(
        member.astype(BF16),
        before.astype(F32).astype(BF16),
        (((1,), (0,)), ((), ())),
        preferred_element_type=F32,
    )
    return hits, jnp.where(member > 0.5, place, -1.0)


def one_hot(place, capacity):
    experts, tokens = place.shape
    spread = jnp.broadcast_to(place[:, None, :], (experts, capacity, tokens))
    slot = lax.broadcasted_iota(jnp.int32, (experts, capacity, tokens), 1).astype(F32)
    return (spread == slot).astype(F32).reshape(experts * capacity, tokens)


def eye(shape):
    return lax.broadcasted_iota(jnp.int32, shape, 1) == lax.broadcasted_iota(jnp.int32, shape, 2)


def to_lanes(column, sources):
    rows = column.shape[0]
    shape = (sources, rows // sources, LANES)
    spread = jnp.broadcast_to(column, (rows, LANES)).reshape(shape)
    return jnp.sum(jnp.where(eye(shape), spread, 0.0), axis=1, keepdims=True)


def to_column(line, capacity):
    sources = line.shape[0]
    shape = (sources, capacity, LANES)
    spread = jnp.where(eye(shape), jnp.broadcast_to(line, shape), 0.0)
    return jnp.sum(spread.reshape(sources * capacity, LANES), axis=1, keepdims=True)


def send_rows(place, tokens_ref, out_ref, base):
    tokens = place.shape[1]
    experts, _, lanes = out_ref.shape
    chosen = one_hot(place, CAPACITY)
    rows = jnp.dot(chosen.astype(BF16), tokens_ref[:tokens, :], preferred_element_type=F32)
    rows = rows.astype(BF16)
    for b in range(rows.shape[1] // lanes):
        start = base + b * CAPACITY
        out_ref[:, start : start + CAPACITY, :] = rows[:, b * lanes : (b + 1) * lanes].reshape(
            experts, CAPACITY, lanes
        )
    return chosen


def dispatch_kernel(got_ref, keep_ref, routes_ref, gate_ref, out_ref):
    experts = out_ref.shape[0]
    height = (out_ref.shape[1] - 8) // 2
    table = got_ref[LANES:, :LANES].astype(F32)
    _, place = places(table[: table.shape[0] // 2], experts)
    send_rows(place, got_ref, out_ref, 0)
    gate = gate_ref[...].astype(F32)
    hits, place = places(routes_ref[...].astype(F32), experts)
    chosen = send_rows(place, keep_ref, out_ref, height)
    gates = functools.reduce(
        jnp.add, [jnp.where(h, gate[k : k + 1, :], 0.0) for k, h in enumerate(hits)]
    )
    spread = jnp.broadcast_to(gates[:, None, :], (experts, CAPACITY, gates.shape[1]))
    column = jnp.sum(chosen * spread.reshape(chosen.shape), axis=1, keepdims=True)
    line = to_lanes(column, experts)
    out_ref[:, 2 * height :, :] = jnp.broadcast_to(line, (experts, 8, LANES)).astype(BF16)


def matmul_kernel(shifts, base, info_ref, arrived_ref, *refs):
    weights, (out_ref, rows_ref) = refs[:-2], refs[-2:]
    parts = [(w, i) for w in weights for i in range(w.shape[0])]

    @pl.when(pl.program_id(0) == 0)
    def _():
        slots = out_ref.shape[0]
        capacity = slots // arrived_ref.shape[0]
        for n, (dz, dx) in enumerate(shifts):
            chip = ((info_ref[1] + dz) & 3) * 4 + ((info_ref[2] + dx) & 3)
            start = pl.multiple_of(base + chip * capacity, capacity)
            rows_ref[:, n * LANES : (n + 1) * LANES] = arrived_ref[
                :, pl.ds(start, capacity), :
            ].reshape(slots, LANES)

    block = jnp.concatenate([w[i] for w, i in parts], axis=1)
    out_ref[...] = lax.dot_general(
        rows_ref[...], block, (((1,), (1,)), ((), ())), preferred_element_type=F32
    )


def finish_kernel(mine_ref, theirs_ref, saved_ref, gate_ref, out_ref, score_ref):
    rows, units = mine_ref.shape
    here = pl.ds(pl.multiple_of(pl.program_id(0) * rows, rows), rows)
    sources = score_ref.shape[0]
    step = 256
    total = jnp.zeros((rows, 1), F32)
    gate_in = to_column(gate_ref[...].astype(F32)[:, :1, :], rows // sources)
    for j in range(units // step):
        cols = slice(j * step, (j + 1) * step)
        up_cols = slice(units + j * step, units + (j + 1) * step)
        grad = mine_ref[:, cols] + theirs_ref[here, cols]
        a = saved_ref[:, cols].astype(F32)
        u = saved_ref[:, up_cols].astype(F32)
        sig = 1.0 / (1.0 + jnp.exp(-a))
        silu = a * sig
        hidden = (silu * u).astype(BF16).astype(F32)
        total += jnp.sum(grad * hidden, axis=1, keepdims=True)
        scaled = grad * gate_in
        out_ref[:, cols] = (scaled * u * sig * (1.0 + a * (1.0 - sig))).astype(BF16)
        out_ref[:, up_cols] = (scaled * silu).astype(BF16)
    score_ref[...] = jnp.broadcast_to(to_lanes(total, sources), score_ref.shape)


def home_kernel(routes_ref, back_ref, out_ref):
    experts = back_ref.shape[0]
    routes = routes_ref[...].astype(F32)
    hits, place = places(routes, experts)
    chosen = one_hot(place, CAPACITY)
    column = to_column(back_ref[:, :1, :], CAPACITY)
    score = jnp.sum((column * chosen).reshape(experts, CAPACITY, -1), axis=1)
    for k, h in enumerate(hits):
        out_ref[k : k + 1, :] = jnp.sum(jnp.where(h, score, 0.0), axis=0, keepdims=True)


def call(kernel, shapes, in_specs, out_specs, scratch=(), grid=()):
    return pl.pallas_call(
        kernel,
        out_shape=shapes,
        grid=grid,
        in_specs=in_specs,
        out_specs=out_specs,
        scratch_shapes=list(scratch),
        compiler_params=pltpu.CompilerParams(vmem_limit_bytes=24 << 20),
    )


def near(array):
    return pltpu.with_memory_space_constraint(array, pltpu.VMEM)


def far(array):
    return pltpu.with_memory_space_constraint(array, pltpu.HBM)


def permute(array, axis, shift):
    return lax.ppermute(array, axis, ring(4, shift))


def gather_weights(block):
    z1, z3, z2 = (permute(block, "zl", r) for r in (1, 3, 2))
    a1, a3 = permute(block, "x", 1), permute(block, "x", 3)
    pair = jnp.concatenate([z1, z3], axis=0)
    g1, g3 = permute(pair, "x", 1), permute(pair, "x", 3)
    a2 = permute(a1, "x", 1)
    h1, h3 = permute(z2, "x", 1), permute(z2, "x", 3)
    f1 = permute(g1[:1], "x", 1)
    f3 = permute(g3[1:], "x", 3)
    f2 = permute(h3, "x", 3)
    groups = [(block, (0,), 0), (a1, (0,), 1), (a3, (0,), 3), (a2, (0,), 2)]
    groups += [(pair, (1, 3), 0), (g1, (1, 3), 1), (g3, (1, 3), 3)]
    groups += [(z2, (2,), 0), (h1, (2,), 1), (h3, (2,), 3)]
    return groups + [(f1, (1,), 2), (f3, (3,), 2), (f2, (2,), 2)]


def step(grad_out, routes, gate, saved, w_down):
    tokens, width = grad_out.shape
    units, slots = w_down.shape[1], saved.shape[2]
    sources = slots // CAPACITY
    groups = gather_weights(w_down)
    info = jnp.stack([lax.axis_index(a) for a in ("c", "zl", "x")]).astype(jnp.int32)
    half = width // 2
    blocks = half // LANES
    routes_t, gate_t = routes.T, gate.T
    keep, send = call(
        pack_kernel,
        (
            jax.ShapeDtypeStruct((tokens, half), BF16),
            jax.ShapeDtypeStruct((tokens + 16, half), BF16),
        ),
        [SMEM, VMEM, VMEM],
        (VMEM, VMEM),
    )(info, far(grad_out), far(routes_t))
    got = lax.ppermute(send, "c", ring(2, 1))
    height = CAPACITY * blocks
    outgoing = call(
        dispatch_kernel,
        jax.ShapeDtypeStruct((sources, 2 * height + 8, LANES), BF16),
        [VMEM] * 4,
        VMEM,
    )(got, keep, far(routes_t), far(gate_t))
    arrived = lax.all_to_all(outgoing, EP, split_axis=0, concat_axis=0, tiled=True)
    part = 512
    piece = pl.BlockSpec((slots, part), lambda j: (0, j))
    shifts = [(dz, dx) for _, dzs, dx in groups for dz in dzs]
    arrays = [a for a, _, _ in groups]

    def product(base):
        return call(
            functools.partial(matmul_kernel, shifts, base),
            jax.ShapeDtypeStruct((slots, units), F32),
            [SMEM, VMEM]
            + [pl.BlockSpec((a.shape[0], part, LANES), lambda j: (0, j, 0)) for a in arrays],
            piece,
            [pltpu.VMEM((slots, half), BF16)],
            (units // part,),
        )(info, near(arrived), *map(far, arrays))

    theirs = product(0)
    mine = product(height)
    theirs = lax.ppermute(theirs, "c", ring(2, 1))
    gates = arrived[:, 2 * height :, :]
    steps = 4
    rows = slots // steps
    tile = pl.BlockSpec((sources // steps, 8, LANES), lambda i: (i, 0, 0))
    wide = pl.BlockSpec((rows, 2 * units), lambda i: (i, 0))
    grad_pre, score = call(
        finish_kernel,
        (
            jax.ShapeDtypeStruct((slots, 2 * units), BF16),
            jax.ShapeDtypeStruct((sources, 8, LANES), F32),
        ),
        [pl.BlockSpec((rows, units), lambda i: (i, 0)), VMEM, wide, tile],
        (wide, tile),
        grid=(steps,),
    )(mine, near(theirs), saved[0, 0], gates)
    back = lax.all_to_all(score, EP, split_axis=0, concat_axis=0, tiled=True)
    grad_gate = call(
        home_kernel, jax.ShapeDtypeStruct((routes.shape[1], tokens), F32), [VMEM, VMEM], VMEM
    )(routes_t, back)
    return grad_pre.reshape(saved.shape), grad_gate.T


def solution(mesh):
    fine = Mesh(mesh.devices.reshape(2, 8, 4, 4, 2), ("zh", "y", "zl", "x", "c"))
    sp = ("zl", "x", "c")
    in_specs = (
        P(EP + sp, None),
        P(EP + sp, None),
        P(EP + sp, None),
        P(EP, sp, None, None),
        P(EP, None, sp),
    )
    out_specs = (P(EP, sp, None, None), P(EP + sp, None))
    return jax.shard_map(step, mesh=fine, in_specs=in_specs, out_specs=out_specs, check_vma=False)
```

time: 216 us -> 206 us (0.954)
  the two profiles are of different devices: /device:TPU:1 before, /device:TPU:198 now
where the time goes in v2:
time: 206 us; the launch traced here: 205 us
  waiting for transfers between devices  85.7 us (42%)
  starting transfers between devices  57.8 us (28%)
  blocking collectives  40.8 us (20%)
  Pallas kernels  16.7 us (8%)
  local copies, waits for them, and re-layouts  3.04 us (1%)
    ppermute x13, waiting for transfers between devices, permute(): return lax.ppermute(array, axis, ring(4, shift))  83.7 us
    all_to_all x1, blocking collectives, step(): back = lax.all_to_all(score, EP, split_axis=0, concat_axis=0, tiled=True)  40.8 us
    ppermute x13, starting transfers between devices, permute(): return lax.ppermute(array, axis, ring(4, shift))  40.7 us
    all_to_all x1, starting transfers between devices, step(): lax.all_to_all(outgoing, EP, split_axis=0, concat_axis=0, tiled=True)  13.1 us
    pallas_call x2, Pallas kernels, product(): call(functools.partial(matmul_kernel, shifts, base), jax.ShapeDtypeStruct...  10.3 us
  transfers between devices with their start and end apart: 16, of which 8 were waited for; matrix products, arithmetic and copies ran while one was open for 0% of the time, Pallas kernels for 3%

profile of v2, /device:TPU:198, one launch (start us, length us, event | category | flops | bytes accessed | tf_op | source)
XLA Modules:
  0.0 205.0 jit_solution(7081624791997712155)
XLA Ops:
  0.6 0.1 pad_add_fusion.core_ref.info_ref
  0.7 1.5 shard_map.68
  2.2 1.9 collective-permute-start
  4.2 2.0 collective-permute-done.got_ref
  6.1 1.6 shard_map.69
  7.8 0.0 copy-start
  7.8 1.3 copy-done
  9.1 13.1 %all-to-all-start = ((bf16[16,520,128]{2,1,0:T(8,128)(2,1)}), bf16[16,520,128]{2,1,0:T(8,128)(2,1)S(1)}, u32[]{:S(2)}, u32[]{:S(2)}) async-start(bf16[16,520,128]{2,1,0:T(8,128)(2,1)} %copy-done), calls=%async_computation | async-start | bytes 4259840 | tf_op jit(solution)/shard_map/all_to_all | solution.py:231
  22.2 2.5 %collective-permute-start.4 = (bf16[1,1536,128]{2,1,0:T(8,128)(2,1)S(1)}, bf16[1,1536,128]{2,1,0:T(8,128)(2,1)S(1)}, u32[]{:S(2)}, u32[]{:S(2)}) collective-permute-start(bf16[1,1536,128]{2,1,0:T(8,128)(2,1)S(1)} %copy-done.6), channel_id=1, source_target_pairs={{8,0},{16,8},{24,16},{0,24},{9,1},{17,9},{25,17},{1,25},{10,2},{18... | collective-permute-start | bytes 1179656 | tf_op jit(solution)/shard_map/ppermute | solution.py:186
  24.7 5.2 %collective-permute-start.5 = (bf16[1,1536,128]{2,1,0:T(8,128)(2,1)S(1)}, bf16[1,1536,128]{2,1,0:T(8,128)(2,1)S(1)}, u32[]{:S(2)}, u32[]{:S(2)}) collective-permute-start(bf16[1,1536,128]{2,1,0:T(8,128)(2,1)S(1)} %copy-done.6), channel_id=1, source_target_pairs={{24,0},{0,8},{8,16},{16,24},{25,1},{1,9},{9,17},{17,25},{26,2},{2,... | collective-permute-start | bytes 1179656 | tf_op jit(solution)/shard_map/ppermute | solution.py:186
  29.9 1.9 collective-permute-start.8
  31.8 51.2 %collective-permute-done.4 = bf16[1,1536,128]{2,1,0:T(8,128)(2,1)S(1)} collective-permute-done((bf16[1,1536,128]{2,1,0:T(8,128)(2,1)S(1)}, bf16[1,1536,128]{2,1,0:T(8,128)(2,1)S(1)}, u32[]{:S(2)}, u32[]{:S(2)}) %collective-permute-start.4) | collective-permute-done | bytes 393248 | tf_op jit(solution)/shard_map/ppermute | solution.py:186
  83.0 3.3 %collective-permute-done.5 = bf16[1,1536,128]{2,1,0:T(8,128)(2,1)S(1)} collective-permute-done((bf16[1,1536,128]{2,1,0:T(8,128)(2,1)S(1)}, bf16[1,1536,128]{2,1,0:T(8,128)(2,1)S(1)}, u32[]{:S(2)}, u32[]{:S(2)}) %collective-permute-start.5) | collective-permute-done | bytes 393248 | tf_op jit(solution)/shard_map/ppermute | solution.py:186
  86.4 0.1 constant_dynamic-update-slice_fusion.refs_4_
  86.4 0.0 copy-start.5
  86.4 2.7 %collective-permute-start.6 = (bf16[2,1536,128]{2,1,0:T(8,128)(2,1)S(1)}, bf16[2,1536,128]{2,1,0:T(8,128)(2,1)S(1)}, u32[]{:S(2)}, u32[]{:S(2)}) collective-permute-start(bf16[2,1536,128]{2,1,0:T(8,128)(2,1)S(1)} %constant_dynamic-update-slice_fusion.refs_4_), channel_id=1, source_target_pairs={{2,0},{4,2},{6,4},{0,6},{3,1},{5,3},{7,5},{1,7},{10,8},{12,10},{14... | collective-permute-start | bytes 2359304 | tf_op jit(solution)/shard_map/ppermute | solution.py:186
  89.2 4.3 %collective-permute-start.7 = (bf16[2,1536,128]{2,1,0:T(8,128)(2,1)S(1)}, bf16[2,1536,128]{2,1,0:T(8,128)(2,1)S(1)}, u32[]{:S(2)}, u32[]{:S(2)}) collective-permute-start(bf16[2,1536,128]{2,1,0:T(8,128)(2,1)S(1)} %constant_dynamic-update-slice_fusion.refs_4_), channel_id=1, source_target_pairs={{6,0},{0,2},{2,4},{4,6},{7,1},{1,3},{3,5},{5,7},{14,8},{8,10},{10,... | collective-permute-start | bytes 2359304 | tf_op jit(solution)/shard_map/ppermute | solution.py:186
  93.5 1.9 collective-permute-start.1
  95.4 8.5 %collective-permute-done.8.refs_7_ = bf16[1,1536,128]{2,1,0:T(8,128)(2,1)S(1)} collective-permute-done((bf16[1,1536,128]{2,1,0:T(8,128)(2,1)S(1)}, bf16[1,1536,128]{2,1,0:T(8,128)(2,1)S(1)}, u32[]{:S(2)}, u32[]{:S(2)}) %collective-permute-start.8) | collective-permute-done | bytes 393248 | tf_op jit(solution)/shard_map/ppermute | solution.py:186
  104.0 2.4 %collective-permute-start.10 = (bf16[1,1536,128]{2,1,0:T(8,128)(2,1)S(1)}, bf16[1,1536,128]{2,1,0:T(8,128)(2,1)S(1)}, u32[]{:S(2)}, u32[]{:S(2)}) collective-permute-start(bf16[1,1536,128]{2,1,0:T(8,128)(2,1)S(1)} %collective-permute-done.8.refs_7_), channel_id=1, source_target_pairs={{6,0},{0,2},{2,4},{4,6},{7,1},{1,3},{3,5},{5,7},{14,8},{8,10},{10,... | collective-permute-start | bytes 1179656 | tf_op jit(solution)/shard_map/ppermute | solution.py:186
  106.4 3.4 %collective-permute-start.2 = (bf16[1,1536,128]{2,1,0:T(8,128)(2,1)S(1)}, bf16[1,1536,128]{2,1,0:T(8,128)(2,1)S(1)}, u32[]{:S(2)}, u32[]{:S(2)}) collective-permute-start(bf16[1,1536,128]{2,1,0:T(8,128)(2,1)S(1)} %copy-done.6), channel_id=1, source_target_pairs={{6,0},{0,2},{2,4},{4,6},{7,1},{1,3},{3,5},{5,7},{14,8},{8,10},{10,... | collective-permute-start | bytes 1179656 | tf_op jit(solution)/shard_map/ppermute | solution.py:186
  109.8 7.4 %collective-permute-done.1.refs_1_ = bf16[1,1536,128]{2,1,0:T(8,128)(2,1)S(1)} collective-permute-done((bf16[1,1536,128]{2,1,0:T(8,128)(2,1)S(1)}, bf16[1,1536,128]{2,1,0:T(8,128)(2,1)S(1)}, u32[]{:S(2)}, u32[]{:S(2)}) %collective-permute-start.1) | collective-permute-done | bytes 393248 | tf_op jit(solution)/shard_map/ppermute | solution.py:186
  117.2 1.9 collective-permute-start.9
  119.1 0.9 collective-permute-done.10.refs_9_
  119.9 2.2 %collective-permute-start.3 = (bf16[1,1536,128]{2,1,0:T(8,128)(2,1)S(1)}, bf16[1,1536,128]{2,1,0:T(8,128)(2,1)S(1)}, u32[]{:S(2)}, u32[]{:S(2)}) collective-permute-start(bf16[1,1536,128]{2,1,0:T(8,128)(2,1)S(1)} %collective-permute-done.1.refs_1_), channel_id=1, source_target_pairs={{2,0},{4,2},{6,4},{0,6},{3,1},{5,3},{7,5},{1,7},{10,8},{12,10},{14... | collective-permute-start | bytes 1179656 | tf_op jit(solution)/shard_map/ppermute | solution.py:186
  122.1 0.0 collective-permute-done.6.refs_5_
  122.1 5.3 %collective-permute-start.13 = (bf16[1,1536,128]{2,1,0:T(8,128)(2,1)S(1)}, bf16[1,1536,128]{2,1,0:T(8,128)(2,1)S(1)}, u32[]{:S(2)}, u32[]{:S(2)}) collective-permute-start(bf16[1,1536,128]{2,1,0:T(8,128)(2,1)S(1)} %collective-permute-done.10.refs_9_), channel_id=1, source_target_pairs={{6,0},{0,2},{2,4},{4,6},{7,1},{1,3},{3,5},{5,7},{14,8},{8,10},{10,... | collective-permute-start | bytes 1179656 | tf_op jit(solution)/shard_map/ppermute | solution.py:186
  127.4 0.0 collective-permute-done.7.refs_6_
  127.5 1.9 collective-permute-start.11
  129.4 0.0 collective-permute-done.2.refs_2_
  129.4 5.1 %collective-permute-start.12 = (bf16[1,1536,128]{2,1,0:T(8,128)(2,1)S(1)}, bf16[1,1536,128]{2,1,0:T(8,128)(2,1)S(1)}, u32[]{:S(2)}, u32[]{:S(2)}) collective-permute-start(bf16[1,1536,128]{2,1,0:T(8,128)(2,1)S(1)} %slice.13), channel_id=1, source_target_pairs={{6,0},{0,2},{2,4},{4,6},{7,1},{1,3},{3,5},{5,7},{14,8},{8,10},{10,... | collective-permute-start | bytes 1179656 | tf_op jit(solution)/shard_map/ppermute | solution.py:186
  134.6 6.1 %collective-permute-done.3.refs_3_ = bf16[1,1536,128]{2,1,0:T(8,128)(2,1)S(1)} collective-permute-done((bf16[1,1536,128]{2,1,0:T(8,128)(2,1)S(1)}, bf16[1,1536,128]{2,1,0:T(8,128)(2,1)S(1)}, u32[]{:S(2)}, u32[]{:S(2)}) %collective-permute-start.3) | collective-permute-done | bytes 393248 | tf_op jit(solution)/shard_map/ppermute | solution.py:186
  140.7 0.0 collective-permute-done.9.refs_8_
  140.7 0.0 collective-permute-done.13.refs_12_
  140.7 6.3 %collective-permute-done.11.refs_10_ = bf16[1,1536,128]{2,1,0:T(8,128)(2,1)S(1)} collective-permute-done((bf16[1,1536,128]{2,1,0:T(8,128)(2,1)S(1)}, bf16[1,1536,128]{2,1,0:T(8,128)(2,1)S(1)}, u32[]{:S(2)}, u32[]{:S(2)}) %collective-permute-start.11) | collective-permute-done | bytes 393248 | tf_op jit(solution)/shard_map/ppermute | solution.py:186
  147.1 0.7 copy-done.14
  147.8 0.0 collective-permute-done.12.refs_11_
  147.8 0.0 all-to-all-done.arrived_ref
  147.8 0.7 copy-done.15
  148.6 5.1 %shard_map.71 = f32[256,1536]{1,0:T(8,128)S(1)} custom-call(s32[3]{0:T(128)S(1)} %pad_add_fusion.core_ref.info_ref, bf16[16,520,128]{2,1,0:T(8,128)(2,1)S(1)} %all-to-all-done.arrived_ref, bf16[1,1536,128]{2,1,0:T(8,128)(2,1)} %refs_0_.3, bf16[1,1536,128]{2,1,0:T(8,128)(2,1)} %copy-done.8, bf16[1,1536,128]{2,1,0:T(8,128)(2,1)} %copy-done.10, ...), custom_call_target="tpu_custom_call" | custom-call | tf_op jit(solution)/shard_map/pallas_call | solution.py:238
  153.7 0.0 copy-start.1
  153.7 2.1 %collective-permute-start.14 = (f32[256,1536]{1,0:T(8,128)S(1)}, f32[256,1536]{1,0:T(8,128)S(1)}, u32[]{:S(2)}, u32[]{:S(2)}) collective-permute-start(f32[256,1536]{1,0:T(8,128)S(1)} %shard_map.71), channel_id=1, source_target_pairs={{1,0},{0,1},{3,2},{2,3},{5,4},{4,5},{7,6},{6,7},{9,8},{8,9},{11,10... | collective-permute-start | bytes 4718600 | tf_op jit(solution)/shard_map/ppermute | solution.py:250
  155.8 5.1 %shard_map.70.mine_ref = f32[256,1536]{1,0:T(8,128)S(1)} custom-call(s32[3]{0:T(128)S(1)} %pad_add_fusion.core_ref.info_ref, bf16[16,520,128]{2,1,0:T(8,128)(2,1)S(1)} %all-to-all-done.arrived_ref, bf16[1,1536,128]{2,1,0:T(8,128)(2,1)} %refs_0_.3, bf16[1,1536,128]{2,1,0:T(8,128)(2,1)} %copy-done.8, bf16[1,1536,128]{2,1,0:T(8,128)(2,1)} %copy-done.10, ...), custom_call_target="tpu_custom_call" | custom-call | tf_op jit(solution)/shard_map/pallas_call | solution.py:238
  161.0 0.0 collective-permute-done.14.theirs_ref
  161.0 0.0 copy-start.2
  161.0 2.5 %shard_map.72 = (bf16[256,3072]{1,0:T(8,128)(2,1)}, f32[16,8,128]{2,1,0:T(8,128)S(1)}) custom-call(f32[256,1536]{1,0:T(8,128)S(1)} %shard_map.70.mine_ref, f32[256,1536]{1,0:T(8,128)S(1)} %collective-permute-done.14.theirs_ref, bf16[256,3072]{1,0:T(8,128)(2,1)S(1)} %bitcast.8, bf16[16,8,128]{2,1,0:T(8,128)(2,1)S(1)} %slice.14.gate_ref), custom_call_target="tpu_custom_call" | custom-call | tf_op jit(solution)/shard_map/pallas_call | solution.py:256
  163.5 40.8 %all_to_all.10.back_ref = f32[16,8,128]{2,1,0:T(8,128)S(1)} all-to-all(f32[16,8,128]{2,1,0:T(8,128)S(1)} %get-tuple-element.9), channel_id=1, replica_groups=mesh['zh'=2,'y'=8,'zl'=4,'x'=4,'c'=2] {'zh','y'}, dimensions={0} | all-to-all | bytes 131072 | tf_op jit(solution)/shard_map/all_to_all | solution.py:266
  204.2 0.8 shard_map.73
  (29 shorter events, 0.1 us)
Async XLA Ops:
  2.2 3.9 %collective-permute-start = (bf16[144,2048]{1,0:T(8,128)(2,1)S(1)}, bf16[144,2048]{1,0:T(8,128)(2,1)S(1)}, u32[]{:S(2)}, u32[]{:S(2)}) collective-permute-start(bf16[144,2048]{1,0:T(8,128)(2,1)S(1)} %get-tuple-element.6), channel_id=1, source_target_pairs={{1,0},{0,1},{3,2},{2,3},{5,4},{4,5},{7,6},{6,7},{9,8},{8,9},{11,10... | collective-permute-start | bytes 1769480 | tf_op jit(solution)/shard_map/ppermute | solution.py:223
  7.8 1.4 copy-start
  9.1 13.1 %copy-start.6 = (bf16[1,1536,128]{2,1,0:T(8,128)(2,1)S(1)}, bf16[1,1536,128]{2,1,0:T(8,128)(2,1)}, u32[]{:S(2)}) copy-start(bf16[1,1536,128]{2,1,0:T(8,128)(2,1)} %refs_0_.3) | copy-start | bytes 1179652
  9.1 138.7 %all-to-all-start = ((bf16[16,520,128]{2,1,0:T(8,128)(2,1)}), bf16[16,520,128]{2,1,0:T(8,128)(2,1)S(1)}, u32[]{:S(2)}, u32[]{:S(2)}) async-start(bf16[16,520,128]{2,1,0:T(8,128)(2,1)} %copy-done), calls=%async_computation | async-start | bytes 4259840 | tf_op jit(solution)/shard_map/all_to_all | solution.py:231
  22.2 60.8 %collective-permute-start.4 = (bf16[1,1536,128]{2,1,0:T(8,128)(2,1)S(1)}, bf16[1,1536,128]{2,1,0:T(8,128)(2,1)S(1)}, u32[]{:S(2)}, u32[]{:S(2)}) collective-permute-start(bf16[1,1536,128]{2,1,0:T(8,128)(2,1)S(1)} %copy-done.6), channel_id=1, source_target_pairs={{8,0},{16,8},{24,16},{0,24},{9,1},{17,9},{25,17},{1,25},{10,2},{18... | collective-permute-start | bytes 1179656 | tf_op jit(solution)/shard_map/ppermute | solution.py:186
  24.7 61.7 %collective-permute-start.5 = (bf16[1,1536,128]{2,1,0:T(8,128)(2,1)S(1)}, bf16[1,1536,128]{2,1,0:T(8,128)(2,1)S(1)}, u32[]{:S(2)}, u32[]{:S(2)}) collective-permute-start(bf16[1,1536,128]{2,1,0:T(8,128)(2,1)S(1)} %copy-done.6), channel_id=1, source_target_pairs={{24,0},{0,8},{8,16},{16,24},{25,1},{1,9},{9,17},{17,25},{26,2},{2,... | collective-permute-start | bytes 1179656 | tf_op jit(solution)/shard_map/ppermute | solution.py:186
  29.9 74.1 %collective-permute-start.8 = (bf16[1,1536,128]{2,1,0:T(8,128)(2,1)S(1)}, bf16[1,1536,128]{2,1,0:T(8,128)(2,1)S(1)}, u32[]{:S(2)}, u32[]{:S(2)}) collective-permute-start(bf16[1,1536,128]{2,1,0:T(8,128)(2,1)S(1)} %copy-done.6), channel_id=1, source_target_pairs={{16,0},{24,8},{0,16},{8,24},{17,1},{25,9},{1,17},{9,25},{18,2},{26... | collective-permute-start | bytes 1179656 | tf_op jit(solution)/shard_map/ppermute | solution.py:186
  86.4 60.6 %copy-start.5 = (bf16[2,1536,128]{2,1,0:T(8,128)(2,1)}, bf16[2,1536,128]{2,1,0:T(8,128)(2,1)S(1)}, u32[]{:S(2)}) copy-start(bf16[2,1536,128]{2,1,0:T(8,128)(2,1)S(1)} %constant_dynamic-update-slice_fusion.refs_4_) | copy-start | bytes 2359300
  86.4 35.6 %collective-permute-start.6 = (bf16[2,1536,128]{2,1,0:T(8,128)(2,1)S(1)}, bf16[2,1536,128]{2,1,0:T(8,128)(2,1)S(1)}, u32[]{:S(2)}, u32[]{:S(2)}) collective-permute-start(bf16[2,1536,128]{2,1,0:T(8,128)(2,1)S(1)} %constant_dynamic-update-slice_fusion.refs_4_), channel_id=1, source_target_pairs={{2,0},{4,2},{6,4},{0,6},{3,1},{5,3},{7,5},{1,7},{10,8},{12,10},{14... | collective-permute-start | bytes 2359304 | tf_op jit(solution)/shard_map/ppermute | solution.py:186
  89.2 38.2 %collective-permute-start.7 = (bf16[2,1536,128]{2,1,0:T(8,128)(2,1)S(1)}, bf16[2,1536,128]{2,1,0:T(8,128)(2,1)S(1)}, u32[]{:S(2)}, u32[]{:S(2)}) collective-permute-start(bf16[2,1536,128]{2,1,0:T(8,128)(2,1)S(1)} %constant_dynamic-update-slice_fusion.refs_4_), channel_id=1, source_target_pairs={{6,0},{0,2},{2,4},{4,6},{7,1},{1,3},{3,5},{5,7},{14,8},{8,10},{10,... | collective-permute-start | bytes 2359304 | tf_op jit(solution)/shard_map/ppermute | solution.py:186
  93.5 23.6 %collective-permute-start.1 = (bf16[1,1536,128]{2,1,0:T(8,128)(2,1)S(1)}, bf16[1,1536,128]{2,1,0:T(8,128)(2,1)S(1)}, u32[]{:S(2)}, u32[]{:S(2)}) collective-permute-start(bf16[1,1536,128]{2,1,0:T(8,128)(2,1)S(1)} %copy-done.6), channel_id=1, source_target_pairs={{2,0},{4,2},{6,4},{0,6},{3,1},{5,3},{7,5},{1,7},{10,8},{12,10},{14... | collective-permute-start | bytes 1179656 | tf_op jit(solution)/shard_map/ppermute | solution.py:186
  104.0 43.0 %copy-start.7 = (bf16[1,1536,128]{2,1,0:T(8,128)(2,1)}, bf16[1,1536,128]{2,1,0:T(8,128)(2,1)S(1)}, u32[]{:S(2)}) copy-start(bf16[1,1536,128]{2,1,0:T(8,128)(2,1)S(1)} %collective-permute-done.8.refs_7_) | copy-start | bytes 1179652
  104.0 16.0 %collective-permute-start.10 = (bf16[1,1536,128]{2,1,0:T(8,128)(2,1)S(1)}, bf16[1,1536,128]{2,1,0:T(8,128)(2,1)S(1)}, u32[]{:S(2)}, u32[]{:S(2)}) collective-permute-start(bf16[1,1536,128]{2,1,0:T(8,128)(2,1)S(1)} %collective-permute-done.8.refs_7_), channel_id=1, source_target_pairs={{6,0},{0,2},{2,4},{4,6},{7,1},{1,3},{3,5},{5,7},{14,8},{8,10},{10,... | collective-permute-start | bytes 1179656 | tf_op jit(solution)/shard_map/ppermute | solution.py:186
  106.4 23.1 %collective-permute-start.2 = (bf16[1,1536,128]{2,1,0:T(8,128)(2,1)S(1)}, bf16[1,1536,128]{2,1,0:T(8,128)(2,1)S(1)}, u32[]{:S(2)}, u32[]{:S(2)}) collective-permute-start(bf16[1,1536,128]{2,1,0:T(8,128)(2,1)S(1)} %copy-done.6), channel_id=1, source_target_pairs={{6,0},{0,2},{2,4},{4,6},{7,1},{1,3},{3,5},{5,7},{14,8},{8,10},{10,... | collective-permute-start | bytes 1179656 | tf_op jit(solution)/shard_map/ppermute | solution.py:186
  117.2 29.8 %copy-start.8 = (bf16[1,1536,128]{2,1,0:T(8,128)(2,1)}, bf16[1,1536,128]{2,1,0:T(8,128)(2,1)S(1)}, u32[]{:S(2)}) copy-start(bf16[1,1536,128]{2,1,0:T(8,128)(2,1)S(1)} %collective-permute-done.1.refs_1_) | copy-start | bytes 1179652
  117.2 23.5 %collective-permute-start.9 = (bf16[1,1536,128]{2,1,0:T(8,128)(2,1)S(1)}, bf16[1,1536,128]{2,1,0:T(8,128)(2,1)S(1)}, u32[]{:S(2)}, u32[]{:S(2)}) collective-permute-start(bf16[1,1536,128]{2,1,0:T(8,128)(2,1)S(1)} %collective-permute-done.8.refs_7_), channel_id=1, source_target_pairs={{2,0},{4,2},{6,4},{0,6},{3,1},{5,3},{7,5},{1,7},{10,8},{12,10},{14... | collective-permute-start | bytes 1179656 | tf_op jit(solution)/shard_map/ppermute | solution.py:186
  119.9 27.1 %copy-start.9 = (bf16[1,1536,128]{2,1,0:T(8,128)(2,1)}, bf16[1,1536,128]{2,1,0:T(8,128)(2,1)S(1)}, u32[]{:S(2)}) copy-start(bf16[1,1536,128]{2,1,0:T(8,128)(2,1)S(1)} %collective-permute-done.10.refs_9_) | copy-start | bytes 1179652
  119.9 20.7 %collective-permute-start.3 = (bf16[1,1536,128]{2,1,0:T(8,128)(2,1)S(1)}, bf16[1,1536,128]{2,1,0:T(8,128)(2,1)S(1)}, u32[]{:S(2)}, u32[]{:S(2)}) collective-permute-start(bf16[1,1536,128]{2,1,0:T(8,128)(2,1)S(1)} %collective-permute-done.1.refs_1_), channel_id=1, source_target_pairs={{2,0},{4,2},{6,4},{0,6},{3,1},{5,3},{7,5},{1,7},{10,8},{12,10},{14... | collective-permute-start | bytes 1179656 | tf_op jit(solution)/shard_map/ppermute | solution.py:186
  122.1 25.7 %copy-start.3 = (bf16[2,1536,128]{2,1,0:T(8,128)(2,1)}, bf16[2,1536,128]{2,1,0:T(8,128)(2,1)S(1)}, u32[]{:S(2)}) copy-start(bf16[2,1536,128]{2,1,0:T(8,128)(2,1)S(1)} %collective-permute-done.6.refs_5_) | copy-start | bytes 2359300
  122.1 18.6 %collective-permute-start.13 = (bf16[1,1536,128]{2,1,0:T(8,128)(2,1)S(1)}, bf16[1,1536,128]{2,1,0:T(8,128)(2,1)S(1)}, u32[]{:S(2)}, u32[]{:S(2)}) collective-permute-start(bf16[1,1536,128]{2,1,0:T(8,128)(2,1)S(1)} %collective-permute-done.10.refs_9_), channel_id=1, source_target_pairs={{6,0},{0,2},{2,4},{4,6},{7,1},{1,3},{3,5},{5,7},{14,8},{8,10},{10,... | collective-permute-start | bytes 1179656 | tf_op jit(solution)/shard_map/ppermute | solution.py:186
  127.4 19.6 %copy-start.4 = (bf16[2,1536,128]{2,1,0:T(8,128)(2,1)}, bf16[2,1536,128]{2,1,0:T(8,128)(2,1)S(1)}, u32[]{:S(2)}) copy-start(bf16[2,1536,128]{2,1,0:T(8,128)(2,1)S(1)} %collective-permute-done.7.refs_6_) | copy-start | bytes 2359300
  127.5 19.5 %collective-permute-start.11 = (bf16[1,1536,128]{2,1,0:T(8,128)(2,1)S(1)}, bf16[1,1536,128]{2,1,0:T(8,128)(2,1)S(1)}, u32[]{:S(2)}, u32[]{:S(2)}) collective-permute-start(bf16[1,1536,128]{2,1,0:T(8,128)(2,1)S(1)} %slice.12), channel_id=1, source_target_pairs={{2,0},{4,2},{6,4},{0,6},{3,1},{5,3},{7,5},{1,7},{10,8},{12,10},{14... | collective-permute-start | bytes 1179656 | tf_op jit(solution)/shard_map/ppermute | solution.py:186
  129.4 17.6 %copy-start.10 = (bf16[1,1536,128]{2,1,0:T(8,128)(2,1)}, bf16[1,1536,128]{2,1,0:T(8,128)(2,1)S(1)}, u32[]{:S(2)}) copy-start(bf16[1,1536,128]{2,1,0:T(8,128)(2,1)S(1)} %collective-permute-done.2.refs_2_) | copy-start | bytes 1179652
  129.4 18.4 %collective-permute-start.12 = (bf16[1,1536,128]{2,1,0:T(8,128)(2,1)S(1)}, bf16[1,1536,128]{2,1,0:T(8,128)(2,1)S(1)}, u32[]{:S(2)}, u32[]{:S(2)}) collective-permute-start(bf16[1,1536,128]{2,1,0:T(8,128)(2,1)S(1)} %slice.13), channel_id=1, source_target_pairs={{6,0},{0,2},{2,4},{4,6},{7,1},{1,3},{3,5},{5,7},{14,8},{8,10},{10,... | collective-permute-start | bytes 1179656 | tf_op jit(solution)/shard_map/ppermute | solution.py:186
  140.7 6.4 %copy-start.12 = (bf16[1,1536,128]{2,1,0:T(8,128)(2,1)}, bf16[1,1536,128]{2,1,0:T(8,128)(2,1)S(1)}, u32[]{:S(2)}) copy-start(bf16[1,1536,128]{2,1,0:T(8,128)(2,1)S(1)} %collective-permute-done.3.refs_3_) | copy-start | bytes 1179652
  140.7 6.4 %copy-start.11 = (bf16[1,1536,128]{2,1,0:T(8,128)(2,1)}, bf16[1,1536,128]{2,1,0:T(8,128)(2,1)S(1)}, u32[]{:S(2)}) copy-start(bf16[1,1536,128]{2,1,0:T(8,128)(2,1)S(1)} %collective-permute-done.9.refs_8_) | copy-start | bytes 1179652
  140.7 6.4 %copy-start.13 = (bf16[1,1536,128]{2,1,0:T(8,128)(2,1)}, bf16[1,1536,128]{2,1,0:T(8,128)(2,1)S(1)}, u32[]{:S(2)}) copy-start(bf16[1,1536,128]{2,1,0:T(8,128)(2,1)S(1)} %collective-permute-done.13.refs_12_) | copy-start | bytes 1179652
  147.1 0.8 copy-start.14
  147.8 0.8 copy-start.15
  153.7 7.3 %copy-start.1 = (bf16[1,1,256,3072]{3,2,1,0:T(8,128)(2,1)S(1)}, bf16[1,1,256,3072]{3,2,1,0:T(8,128)(2,1)}, u32[]{:S(2)}) copy-start(bf16[1,1,256,3072]{3,2,1,0:T(8,128)(2,1)} %param.8) | copy-start | bytes 4718596
  153.7 7.2 %collective-permute-start.14 = (f32[256,1536]{1,0:T(8,128)S(1)}, f32[256,1536]{1,0:T(8,128)S(1)}, u32[]{:S(2)}, u32[]{:S(2)}) collective-permute-start(f32[256,1536]{1,0:T(8,128)S(1)} %shard_map.71), channel_id=1, source_target_pairs={{1,0},{0,1},{3,2},{2,3},{5,4},{4,5},{7,6},{6,7},{9,8},{8,9},{11,10... | collective-permute-start | bytes 4718600 | tf_op jit(solution)/shard_map/ppermute | solution.py:250
  161.0 43.3 %copy-start.2 = (s32[128,8]{0,1:T(8,128)S(1)}, s32[128,8]{0,1:T(8,128)}, u32[]{:S(2)}) copy-start(s32[128,8]{0,1:T(8,128)} %param.6) | copy-start | bytes 12292

commit v3 on v2

--- a/solution.py
+++ b/solution.py
@@ -12,6 +12,7 @@
 CAPACITY = 16
 STEP = 8
 EP = ("zh", "y")
+STAY, CROSS = 3, 4
 F32, BF16 = jnp.float32, jnp.bfloat16
 VMEM = pl.BlockSpec(memory_space=pltpu.VMEM)
 SMEM = pl.BlockSpec(memory_space=pltpu.SMEM)
@@ -33,9 +34,9 @@
     send_ref[rows:, :LANES] = jnp.concatenate([routes, routes], axis=0).astype(BF16)
 
 
-def places(routes, experts):
+def places(routes, experts, first=0):
     tokens = routes.shape[1]
-    wanted = (STEP * lax.broadcasted_iota(jnp.int32, (experts, tokens), 0)).astype(F32)
+    wanted = (STEP * (lax.broadcasted_iota(jnp.int32, (experts, tokens), 0) + first)).astype(F32)
     hits = [routes[k : k + 1, :] == wanted for k in range(routes.shape[0])]
     member = functools.reduce(jnp.add, [h.astype(F32) for h in hits])
     before = lax.broadcasted_iota(jnp.int32, (tokens, tokens), 0) < lax.broadcasted_iota(
@@ -89,14 +90,15 @@
     return chosen
 
 
-def dispatch_kernel(got_ref, keep_ref, routes_ref, gate_ref, out_ref):
+def dispatch_kernel(side, info_ref, got_ref, keep_ref, routes_ref, gate_ref, out_ref):
     experts = out_ref.shape[0]
+    first = info_ref[side] * experts
     height = (out_ref.shape[1] - 8) // 2
     table = got_ref[LANES:, :LANES].astype(F32)
-    _, place = places(table[: table.shape[0] // 2], experts)
+    _, place = places(table[: table.shape[0] // 2], experts, first)
     send_rows(place, got_ref, out_ref, 0)
     gate = gate_ref[...].astype(F32)
-    hits, place = places(routes_ref[...].astype(F32), experts)
+    hits, place = places(routes_ref[...].astype(F32), experts, first)
     chosen = send_rows(place, keep_ref, out_ref, height)
     gates = functools.reduce(
         jnp.add, [jnp.where(h, gate[k : k + 1, :], 0.0) for k, h in enumerate(hits)]
@@ -107,28 +109,32 @@
     out_ref[:, 2 * height :, :] = jnp.broadcast_to(line, (experts, 8, LANES)).astype(BF16)
 
 
-def matmul_kernel(shifts, base, info_ref, arrived_ref, *refs):
-    weights, (out_ref, rows_ref) = refs[:-2], refs[-2:]
+def matmul_kernel(shifts, bases, info_ref, arrived_ref, *refs):
+    weights, outs, rows_ref = refs[: -1 - len(bases)], refs[-1 - len(bases) : -1], refs[-1]
     parts = [(w, i) for w in weights for i in range(w.shape[0])]
+    slots = outs[0].shape[0]
 
     @pl.when(pl.program_id(0) == 0)
     def _():
-        slots = out_ref.shape[0]
         capacity = slots // arrived_ref.shape[0]
         for n, (dz, dx) in enumerate(shifts):
             chip = ((info_ref[1] + dz) & 3) * 4 + ((info_ref[2] + dx) & 3)
-            start = pl.multiple_of(base + chip * capacity, capacity)
-            rows_ref[:, n * LANES : (n + 1) * LANES] = arrived_ref[
-                :, pl.ds(start, capacity), :
-            ].reshape(slots, LANES)
+            for m, base in enumerate(bases):
+                start = pl.multiple_of(base + chip * capacity, capacity)
+                rows_ref[m * slots : (m + 1) * slots, n * LANES : (n + 1) * LANES] = arrived_ref[
+                    :, pl.ds(start, capacity), :
+                ].reshape(slots, LANES)
 
     block = jnp.concatenate([w[i] for w, i in parts], axis=1)
-    out_ref[...] = lax.dot_general(
+    out = lax.dot_general(
         rows_ref[...], block, (((1,), (1,)), ((), ())), preferred_element_type=F32
     )
-
-
-def finish_kernel(mine_ref, theirs_ref, saved_ref, gate_ref, out_ref, score_ref):
+    for m, ref in enumerate(outs):
+        ref[...] = out[m * slots : (m + 1) * slots]
+
+
+def finish_kernel(info_ref, mine_ref, theirs_ref, saved_ref, gate_ref, *refs):
+    out_ref, score_ref = refs[-2:]
     rows, units = mine_ref.shape
     here = pl.ds(pl.multiple_of(pl.program_id(0) * rows, rows), rows)
     sources = score_ref.shape[0]
@@ -162,14 +168,18 @@
         out_ref[k : k + 1, :] = jnp.sum(jnp.where(h, score, 0.0), axis=0, keepdims=True)
 
 
-def call(kernel, shapes, in_specs, out_specs, scratch=(), grid=()):
+def call(kernel, shapes, in_specs, out_specs, scratch=(), grid=(), prefetch=0, aliases=None):
     return pl.pallas_call(
         kernel,
         out_shape=shapes,
-        grid=grid,
-        in_specs=in_specs,
-        out_specs=out_specs,
-        scratch_shapes=list(scratch),
+        grid_spec=pltpu.PrefetchScalarGridSpec(
+            num_scalar_prefetch=prefetch,
+            grid=grid,
+            in_specs=in_specs,
+            out_specs=out_specs,
+            scratch_shapes=list(scratch),
+        ),
+        input_output_aliases=aliases or {},
         compiler_params=pltpu.CompilerParams(vmem_limit_bytes=24 << 20),
     )
 
@@ -207,7 +217,9 @@
     units, slots = w_down.shape[1], saved.shape[2]
     sources = slots // CAPACITY
     groups = gather_weights(w_down)
-    info = jnp.stack([lax.axis_index(a) for a in ("c", "zl", "x")]).astype(jnp.int32)
+    info = jnp.stack(
+        [lax.axis_index(a) for a in ("c", "zl", "x", "zh")] + [1 - lax.axis_index("zh")]
+    ).astype(jnp.int32)
     half = width // 2
     blocks = half // LANES
     routes_t, gate_t = routes.T, gate.T
@@ -222,47 +234,75 @@
     )(info, far(grad_out), far(routes_t))
     got = lax.ppermute(send, "c", ring(2, 1))
     height = CAPACITY * blocks
-    outgoing = call(
-        dispatch_kernel,
-        jax.ShapeDtypeStruct((sources, 2 * height + 8, LANES), BF16),
-        [VMEM] * 4,
-        VMEM,
-    )(got, keep, far(routes_t), far(gate_t))
-    arrived = lax.all_to_all(outgoing, EP, split_axis=0, concat_axis=0, tiled=True)
+    peers = sources // 2
+
+    def outgoing(side):
+        return call(
+            functools.partial(dispatch_kernel, side),
+            jax.ShapeDtypeStruct((peers, 2 * height + 8, LANES), BF16),
+            [SMEM] + [VMEM] * 4,
+            VMEM,
+        )(info, got, keep, far(routes_t), far(gate_t))
+
+    def along_y(array):
+        return lax.all_to_all(array, "y", split_axis=0, concat_axis=0, tiled=True)
+
+    cross = along_y(outgoing(CROSS))
+    cross = lax.ppermute(cross, "zh", ring(2, 1))
+    stay = along_y(outgoing(STAY))
     part = 512
+    slots = slots // 2
     piece = pl.BlockSpec((slots, part), lambda j: (0, j))
     shifts = [(dz, dx) for _, dzs, dx in groups for dz in dzs]
     arrays = [a for a, _, _ in groups]
 
-    def product(base):
+    def products(arrived, *bases):
         return call(
-            functools.partial(matmul_kernel, shifts, base),
-            jax.ShapeDtypeStruct((slots, units), F32),
+            functools.partial(matmul_kernel, shifts, bases),
+            (jax.ShapeDtypeStruct((slots, units), F32),) * len(bases),
             [SMEM, VMEM]
             + [pl.BlockSpec((a.shape[0], part, LANES), lambda j: (0, j, 0)) for a in arrays],
-            piece,
-            [pltpu.VMEM((slots, half), BF16)],
+            (piece,) * len(bases),
+            [pltpu.VMEM((len(bases) * slots, half), BF16)],
             (units // part,),
         )(info, near(arrived), *map(far, arrays))
 
-    theirs = product(0)
-    mine = product(height)
-    theirs = lax.ppermute(theirs, "c", ring(2, 1))
-    gates = arrived[:, 2 * height :, :]
-    steps = 4
+    steps = 2
     rows = slots // steps
-    tile = pl.BlockSpec((sources // steps, 8, LANES), lambda i: (i, 0, 0))
-    wide = pl.BlockSpec((rows, 2 * units), lambda i: (i, 0))
-    grad_pre, score = call(
-        finish_kernel,
-        (
-            jax.ShapeDtypeStruct((slots, 2 * units), BF16),
-            jax.ShapeDtypeStruct((sources, 8, LANES), F32),
-        ),
-        [pl.BlockSpec((rows, units), lambda i: (i, 0)), VMEM, wide, tile],
-        (wide, tile),
-        grid=(steps,),
-    )(mine, near(theirs), saved[0, 0], gates)
+
+    def finish(side, arrived, mine, theirs, *before):
+        tile = (peers // steps, 8, LANES)
+        wide = pl.BlockSpec((rows, 2 * units), lambda i, info: (steps * info[side] + i, 0))
+        score = pl.BlockSpec(tile, lambda i, info: (steps * info[side] + i, 0, 0))
+        return call(
+            finish_kernel,
+            (
+                jax.ShapeDtypeStruct((2 * slots, 2 * units), BF16),
+                jax.ShapeDtypeStruct((sources, 8, LANES), F32),
+            ),
+            [
+                pl.BlockSpec((rows, units), lambda i, info: (i, 0)),
+                VMEM,
+                wide,
+                pl.BlockSpec(tile, lambda i, info: (i, 0, 0)),
+            ]
+            + [pl.BlockSpec(memory_space=pl.ANY)] * len(before),
+            (wide, score),
+            grid=(steps,),
+            prefetch=1,
+            aliases={5 + n: n for n in range(len(before))},
+        )(info, mine, near(theirs), saved[0, 0], arrived[:, 2 * height :, :], *before)
+
+    def swap(array):
+        return lax.ppermute(array, "c", ring(2, 1))
+
+    theirs, mine = products(stay, 0, height)
+    theirs = swap(theirs)
+    before = finish(STAY, stay, mine, theirs)
+    (theirs,) = products(cross, 0)
+    theirs = swap(theirs)
+    (mine,) = products(cross, height)
+    grad_pre, score = finish(CROSS, cross, mine, theirs, *before)
     back = lax.all_to_all(score, EP, split_axis=0, concat_axis=0, tiled=True)
     grad_gate = call(
         home_kernel, jax.ShapeDtypeStruct((routes.shape[1], tokens), F32), [VMEM, VMEM], VMEM

time: 206 us -> 212 us (1.029)
  the two profiles are of different devices: /device:TPU:198 before, /device:TPU:1 now
where the time goes in v3:
time: 212 us; the launch traced here: 211 us
  starting transfers between devices  114 us (54%)
  blocking collectives  37.1 us (18%)
  waiting for transfers between devices  31.3 us (15%)
  Pallas kernels  26.3 us (12%)
    ppermute x13, starting transfers between devices, permute(): return lax.ppermute(array, axis, ring(4, shift))  79.6 us
    all_to_all x1, blocking collectives, step(): back = lax.all_to_all(score, EP, split_axis=0, concat_axis=0, tiled=True)  37.1 us
    all_to_all x2, waiting for transfers between devices, along_y(): return lax.all_to_all(array, 'y', split_axis=0, concat_axis=0, tiled=True)  20.5 us
    pallas_call x3, Pallas kernels, products(): call(functools.partial(matmul_kernel, shifts, bases), (jax.ShapeDtypeStru...  15.4 us
    ppermute x13, waiting for transfers between devices, permute(): return lax.ppermute(array, axis, ring(4, shift))  9.21 us
    ppermute x2, starting transfers between devices, swap(): return lax.ppermute(array, 'c', ring(2, 1))  9.06 us
    ppermute x1, starting transfers between devices, step(): cross = lax.ppermute(cross, 'zh', ring(2, 1))  8.84 us
    ppermute x1, starting transfers between devices, step(): got = lax.ppermute(send, 'c', ring(2, 1))  8.75 us
  transfers between devices with their start and end apart: 19, of which 4 were waited for; matrix products, arithmetic and copies ran while one was open for 0% of the time, Pallas kernels for 9%

profile of v3, /device:TPU:1, one launch (start us, length us, event | category | flops | bytes accessed | tf_op | source)
XLA Modules:
  0.0 211.1 jit_solution(11524209873634122515)
XLA Ops:
  0.6 0.1 stack.23.core_ref.info_ref
  0.7 1.5 shard_map.68
  2.2 8.7 %collective-permute-start = (bf16[144,2048]{1,0:T(8,128)(2,1)S(1)}, bf16[144,2048]{1,0:T(8,128)(2,1)S(1)}, u32[]{:S(2)}, u32[]{:S(2)}) collective-permute-start(bf16[144,2048]{1,0:T(8,128)(2,1)S(1)} %get-tuple-element.10), channel_id=1, source_target_pairs={{1,0},{0,1},{3,2},{2,3},{5,4},{4,5},{7,6},{6,7},{9,8},{8,9},{11,10... | collective-permute-start | bytes 1769480 | tf_op jit(solution)/shard_map/ppermute | solution.py:235
  11.0 1.6 collective-permute-done.got_ref
  12.6 2.4 %shard_map.69 = bf16[8,520,128]{2,1,0:T(8,128)(2,1)} custom-call(s32[5]{0:T(128)S(1)} %stack.23.core_ref.info_ref, bf16[144,2048]{1,0:T(8,128)(2,1)S(1)} %collective-permute-done.got_ref, bf16[128,2048]{1,0:T(8,128)(2,1)S(1)} %get-tuple-element.11.keep_ref, s32[8,128]{1,0:T(8,128)} %bitcast.13, bf16[8,128]{1,0:T(8,128)(2,1)} %bitcast.17), custom_call_target="tpu_custom_call" | custom-call | tf_op jit(solution)/shard_map/pallas_call | solution.py:240
  15.0 4.4 %all-to-all-start = ((bf16[8,520,128]{2,1,0:T(8,128)(2,1)}), bf16[8,520,128]{2,1,0:T(8,128)(2,1)}, u32[]{:S(2)}, u32[]{:S(2)}) async-start(bf16[8,520,128]{2,1,0:T(8,128)(2,1)} %shard_map.69), calls=%async_computation | async-start | bytes 2129920 | tf_op jit(solution)/shard_map/all_to_all | solution.py:248
  19.4 4.8 %collective-permute-start.5 = (bf16[1,1536,128]{2,1,0:T(8,128)(2,1)S(1)}, bf16[1,1536,128]{2,1,0:T(8,128)(2,1)S(1)}, u32[]{:S(2)}, u32[]{:S(2)}) collective-permute-start(bf16[1,1536,128]{2,1,0:T(8,128)(2,1)S(1)} %copy-done.5), channel_id=1, source_target_pairs={{8,0},{16,8},{24,16},{0,24},{9,1},{17,9},{25,17},{1,25},{10,2},{18... | collective-permute-start | bytes 1179656 | tf_op jit(solution)/shard_map/ppermute | solution.py:196
  24.2 1.9 collective-permute-start.6
  26.1 2.4 %shard_map.72 = bf16[8,520,128]{2,1,0:T(8,128)(2,1)} custom-call(s32[5]{0:T(128)S(1)} %stack.23.core_ref.info_ref, bf16[144,2048]{1,0:T(8,128)(2,1)S(1)} %collective-permute-done.got_ref, bf16[128,2048]{1,0:T(8,128)(2,1)S(1)} %get-tuple-element.11.keep_ref, s32[8,128]{1,0:T(8,128)} %bitcast.14, bf16[8,128]{1,0:T(8,128)(2,1)} %bitcast.18), custom_call_target="tpu_custom_call" | custom-call | tf_op jit(solution)/shard_map/pallas_call | solution.py:240
  28.5 20.5 %all-to-all-done = bf16[8,520,128]{2,1,0:T(8,128)(2,1)} async-done(((bf16[8,520,128]{2,1,0:T(8,128)(2,1)}), bf16[8,520,128]{2,1,0:T(8,128)(2,1)}, u32[]{:S(2)}, u32[]{:S(2)}) %all-to-all-start) | async-done | bytes 1064992 | tf_op jit(solution)/shard_map/all_to_all | solution.py:248
  49.0 3.6 %all-to-all-start.1 = ((bf16[8,520,128]{2,1,0:T(8,128)(2,1)}), bf16[8,520,128]{2,1,0:T(8,128)(2,1)S(1)}, u32[]{:S(2)}, u32[]{:S(2)}) async-start(bf16[8,520,128]{2,1,0:T(8,128)(2,1)} %shard_map.72), calls=%async_computation.1 | async-start | bytes 2129920 | tf_op jit(solution)/shard_map/all_to_all | solution.py:248
  52.6 0.0 collective-permute-done.6
  52.6 0.1 constant_dynamic-update-slice_fusion.refs_4_
  52.7 1.9 collective-permute-start.8
  54.6 4.3 %collective-permute-start.9 = (bf16[1,1536,128]{2,1,0:T(8,128)(2,1)S(1)}, bf16[1,1536,128]{2,1,0:T(8,128)(2,1)S(1)}, u32[]{:S(2)}, u32[]{:S(2)}) collective-permute-start(bf16[1,1536,128]{2,1,0:T(8,128)(2,1)S(1)} %copy-done.5), channel_id=1, source_target_pairs={{16,0},{24,8},{0,16},{8,24},{17,1},{25,9},{1,17},{9,25},{18,2},{26... | collective-permute-start | bytes 1179656 | tf_op jit(solution)/shard_map/ppermute | solution.py:196
  58.9 3.4 %collective-permute-start.7 = (bf16[2,1536,128]{2,1,0:T(8,128)(2,1)S(1)}, bf16[2,1536,128]{2,1,0:T(8,128)(2,1)S(1)}, u32[]{:S(2)}, u32[]{:S(2)}) collective-permute-start(bf16[2,1536,128]{2,1,0:T(8,128)(2,1)S(1)} %constant_dynamic-update-slice_fusion.refs_4_), channel_id=1, source_target_pairs={{2,0},{4,2},{6,4},{0,6},{3,1},{5,3},{7,5},{1,7},{10,8},{12,10},{14... | collective-permute-start | bytes 2359304 | tf_op jit(solution)/shard_map/ppermute | solution.py:196
  62.3 3.2 %collective-permute-start.2 = (bf16[1,1536,128]{2,1,0:T(8,128)(2,1)S(1)}, bf16[1,1536,128]{2,1,0:T(8,128)(2,1)S(1)}, u32[]{:S(2)}, u32[]{:S(2)}) collective-permute-start(bf16[1,1536,128]{2,1,0:T(8,128)(2,1)S(1)} %copy-done.5), channel_id=1, source_target_pairs={{2,0},{4,2},{6,4},{0,6},{3,1},{5,3},{7,5},{1,7},{10,8},{12,10},{14... | collective-permute-start | bytes 1179656 | tf_op jit(solution)/shard_map/ppermute | solution.py:196
  65.5 8.8 %collective-permute-start.1 = (bf16[8,520,128]{2,1,0:T(8,128)(2,1)}, bf16[8,520,128]{2,1,0:T(8,128)(2,1)S(1)}, u32[]{:S(2)}, u32[]{:S(2)}) collective-permute-start(bf16[8,520,128]{2,1,0:T(8,128)(2,1)} %all-to-all-done), channel_id=1, source_target_pairs={{256,0},{0,256},{257,1},{1,257},{258,2},{2,258},{259,3},{3,259},{2... | collective-permute-start | bytes 3194888 | tf_op jit(solution)/shard_map/ppermute | solution.py:251
  74.3 1.7 collective-permute-done.9.refs_7_
  76.1 30.4 %collective-permute-start.11 = (bf16[1,1536,128]{2,1,0:T(8,128)(2,1)S(1)}, bf16[1,1536,128]{2,1,0:T(8,128)(2,1)S(1)}, u32[]{:S(2)}, u32[]{:S(2)}) collective-permute-start(bf16[1,1536,128]{2,1,0:T(8,128)(2,1)S(1)} %collective-permute-done.9.refs_7_), channel_id=1, source_target_pairs={{6,0},{0,2},{2,4},{4,6},{7,1},{1,3},{3,5},{5,7},{14,8},{8,10},{10,... | collective-permute-start | bytes 1179656 | tf_op jit(solution)/shard_map/ppermute | solution.py:196
  106.4 0.0 collective-permute-done.2.refs_1_
  106.5 11.2 %collective-permute-start.3 = (bf16[1,1536,128]{2,1,0:T(8,128)(2,1)S(1)}, bf16[1,1536,128]{2,1,0:T(8,128)(2,1)S(1)}, u32[]{:S(2)}, u32[]{:S(2)}) collective-permute-start(bf16[1,1536,128]{2,1,0:T(8,128)(2,1)S(1)} %copy-done.5), channel_id=1, source_target_pairs={{6,0},{0,2},{2,4},{4,6},{7,1},{1,3},{3,5},{5,7},{14,8},{8,10},{10,... | collective-permute-start | bytes 1179656 | tf_op jit(solution)/shard_map/ppermute | solution.py:196
  117.7 1.9 collective-permute-start.10
  119.6 0.0 collective-permute-done.11.refs_9_
  119.7 6.4 %collective-permute-start.4 = (bf16[1,1536,128]{2,1,0:T(8,128)(2,1)S(1)}, bf16[1,1536,128]{2,1,0:T(8,128)(2,1)S(1)}, u32[]{:S(2)}, u32[]{:S(2)}) collective-permute-start(bf16[1,1536,128]{2,1,0:T(8,128)(2,1)S(1)} %collective-permute-done.2.refs_1_), channel_id=1, source_target_pairs={{2,0},{4,2},{6,4},{0,6},{3,1},{5,3},{7,5},{1,7},{10,8},{12,10},{14... | collective-permute-start | bytes 1179656 | tf_op jit(solution)/shard_map/ppermute | solution.py:196
  126.0 1.9 collective-permute-start.14
  128.0 0.0 collective-permute-done.3.refs_2_
  128.0 4.8 %collective-permute-start.13 = (bf16[1,1536,128]{2,1,0:T(8,128)(2,1)S(1)}, bf16[1,1536,128]{2,1,0:T(8,128)(2,1)S(1)}, u32[]{:S(2)}, u32[]{:S(2)}) collective-permute-start(bf16[1,1536,128]{2,1,0:T(8,128)(2,1)S(1)} %slice.17), channel_id=1, source_target_pairs={{6,0},{0,2},{2,4},{4,6},{7,1},{1,3},{3,5},{5,7},{14,8},{8,10},{10,... | collective-permute-start | bytes 1179656 | tf_op jit(solution)/shard_map/ppermute | solution.py:196
  132.8 0.0 collective-permute-done.10.refs_8_
  132.8 3.6 %collective-permute-start.12 = (bf16[1,1536,128]{2,1,0:T(8,128)(2,1)S(1)}, bf16[1,1536,128]{2,1,0:T(8,128)(2,1)}, u32[]{:S(2)}, u32[]{:S(2)}) collective-permute-start(bf16[1,1536,128]{2,1,0:T(8,128)(2,1)S(1)} %slice.16), channel_id=1, source_target_pairs={{2,0},{4,2},{6,4},{0,6},{3,1},{5,3},{7,5},{1,7},{10,8},{12,10},{14... | collective-permute-start | bytes 1179656 | tf_op jit(solution)/shard_map/ppermute | solution.py:196
  136.4 0.0 collective-permute-done.4.refs_3_
  136.4 7.4 %collective-permute-done.13.refs_11_ = bf16[1,1536,128]{2,1,0:T(8,128)(2,1)S(1)} collective-permute-done((bf16[1,1536,128]{2,1,0:T(8,128)(2,1)S(1)}, bf16[1,1536,128]{2,1,0:T(8,128)(2,1)S(1)}, u32[]{:S(2)}, u32[]{:S(2)}) %collective-permute-start.13) | collective-permute-done | bytes 393248 | tf_op jit(solution)/shard_map/ppermute | solution.py:196
  144.0 0.0 collective-permute-done.12.refs_10_
  144.0 0.7 copy-done.13
  144.7 5.1 %shard_map.73 = (f32[128,1536]{1,0:T(8,128)S(1)}, f32[128,1536]{1,0:T(8,128)S(1)}) custom-call(s32[5]{0:T(128)S(1)} %stack.23.core_ref.info_ref, bf16[8,520,128]{2,1,0:T(8,128)(2,1)S(1)} %all-to-all-done.1.arrived_ref, bf16[1,1536,128]{2,1,0:T(8,128)(2,1)} %refs_0_.5, bf16[1,1536,128]{2,1,0:T(8,128)(2,1)} %copy-done.7, bf16[1,1536,128]{2,1,0:T(8,128)(2,1)} %copy-done.9, ...), custom_call_target="tpu_custom_call" | custom-call | tf_op jit(solution)/shard_map/pallas_call | solution.py:260
  149.8 7.1 %collective-permute-start.16 = (f32[128,1536]{1,0:T(8,128)S(1)}, f32[128,1536]{1,0:T(8,128)S(1)}, u32[]{:S(2)}, u32[]{:S(2)}) collective-permute-start(f32[128,1536]{1,0:T(8,128)S(1)} %get-tuple-element.13), channel_id=1, source_target_pairs={{1,0},{0,1},{3,2},{2,3},{5,4},{4,5},{7,6},{6,7},{9,8},{8,9},{11,10... | collective-permute-start | bytes 2359304 | tf_op jit(solution)/shard_map/ppermute | solution.py:297
  157.0 0.0 collective-permute-done.1.arrived_ref
  157.0 0.0 copy-start
  157.0 5.2 %shard_map.71 = f32[128,1536]{1,0:T(8,128)S(1)} custom-call(s32[5]{0:T(128)S(1)} %stack.23.core_ref.info_ref, bf16[8,520,128]{2,1,0:T(8,128)(2,1)S(1)} %collective-permute-done.1.arrived_ref, bf16[1,1536,128]{2,1,0:T(8,128)(2,1)} %refs_0_.5, bf16[1,1536,128]{2,1,0:T(8,128)(2,1)} %copy-done.7, bf16[1,1536,128]{2,1,0:T(8,128)(2,1)} %copy-done.9, ...), custom_call_target="tpu_custom_call" | custom-call | tf_op jit(solution)/shard_map/pallas_call | solution.py:260
  162.2 1.9 collective-permute-start.15
  164.1 0.0 collective-permute-done.16.theirs_ref
  164.1 2.0 shard_map.74
  166.1 5.1 %shard_map.70.mine_ref = f32[128,1536]{1,0:T(8,128)S(1)} custom-call(s32[5]{0:T(128)S(1)} %stack.23.core_ref.info_ref, bf16[8,520,128]{2,1,0:T(8,128)(2,1)S(1)} %collective-permute-done.1.arrived_ref, bf16[1,1536,128]{2,1,0:T(8,128)(2,1)} %refs_0_.5, bf16[1,1536,128]{2,1,0:T(8,128)(2,1)} %copy-done.7, bf16[1,1536,128]{2,1,0:T(8,128)(2,1)} %copy-done.9, ...), custom_call_target="tpu_custom_call" | custom-call | tf_op jit(solution)/shard_map/pallas_call | solution.py:260
  171.2 0.0 collective-permute-done.15.theirs_ref
  171.2 0.0 copy-start.1
  171.2 2.0 shard_map.75
  173.2 37.1 %all_to_all.15.back_ref = f32[16,8,128]{2,1,0:T(8,128)S(1)} all-to-all(f32[16,8,128]{2,1,0:T(8,128)S(1)} %get-tuple-element.17), channel_id=1, replica_groups=mesh['zh'=2,'y'=8,'zl'=4,'x'=4,'c'=2] {'zh','y'}, dimensions={0} | all-to-all | bytes 131072 | tf_op jit(solution)/shard_map/all_to_all | solution.py:306
  210.3 0.8 shard_map.76
  (35 shorter events, 0.2 us)
Async XLA Ops:
  2.2 10.4 %collective-permute-start = (bf16[144,2048]{1,0:T(8,128)(2,1)S(1)}, bf16[144,2048]{1,0:T(8,128)(2,1)S(1)}, u32[]{:S(2)}, u32[]{:S(2)}) collective-permute-start(bf16[144,2048]{1,0:T(8,128)(2,1)S(1)} %get-tuple-element.10), channel_id=1, source_target_pairs={{1,0},{0,1},{3,2},{2,3},{5,4},{4,5},{7,6},{6,7},{9,8},{8,9},{11,10... | collective-permute-start | bytes 1769480 | tf_op jit(solution)/shard_map/ppermute | solution.py:235
  15.0 4.4 %copy-start.5 = (bf16[1,1536,128]{2,1,0:T(8,128)(2,1)S(1)}, bf16[1,1536,128]{2,1,0:T(8,128)(2,1)}, u32[]{:S(2)}) copy-start(bf16[1,1536,128]{2,1,0:T(8,128)(2,1)} %refs_0_.5) | copy-start | bytes 1179652
  15.0 34.0 %all-to-all-start = ((bf16[8,520,128]{2,1,0:T(8,128)(2,1)}), bf16[8,520,128]{2,1,0:T(8,128)(2,1)}, u32[]{:S(2)}, u32[]{:S(2)}) async-start(bf16[8,520,128]{2,1,0:T(8,128)(2,1)} %shard_map.69), calls=%async_computation | async-start | bytes 2129920 | tf_op jit(solution)/shard_map/all_to_all | solution.py:248
  19.4 33.2 %collective-permute-start.5 = (bf16[1,1536,128]{2,1,0:T(8,128)(2,1)S(1)}, bf16[1,1536,128]{2,1,0:T(8,128)(2,1)S(1)}, u32[]{:S(2)}, u32[]{:S(2)}) collective-permute-start(bf16[1,1536,128]{2,1,0:T(8,128)(2,1)S(1)} %copy-done.5), channel_id=1, source_target_pairs={{8,0},{16,8},{24,16},{0,24},{9,1},{17,9},{25,17},{1,25},{10,2},{18... | collective-permute-start | bytes 1179656 | tf_op jit(solution)/shard_map/ppermute | solution.py:196
  24.2 28.4 %collective-permute-start.6 = (bf16[1,1536,128]{2,1,0:T(8,128)(2,1)S(1)}, bf16[1,1536,128]{2,1,0:T(8,128)(2,1)S(1)}, u32[]{:S(2)}, u32[]{:S(2)}) collective-permute-start(bf16[1,1536,128]{2,1,0:T(8,128)(2,1)S(1)} %copy-done.5), channel_id=1, source_target_pairs={{24,0},{0,8},{8,16},{16,24},{25,1},{1,9},{9,17},{17,25},{26,2},{2,... | collective-permute-start | bytes 1179656 | tf_op jit(solution)/shard_map/ppermute | solution.py:196
  49.0 95.0 %all-to-all-start.1 = ((bf16[8,520,128]{2,1,0:T(8,128)(2,1)}), bf16[8,520,128]{2,1,0:T(8,128)(2,1)S(1)}, u32[]{:S(2)}, u32[]{:S(2)}) async-start(bf16[8,520,128]{2,1,0:T(8,128)(2,1)} %shard_map.72), calls=%async_computation.1 | async-start | bytes 2129920 | tf_op jit(solution)/shard_map/all_to_all | solution.py:248
  52.7 91.2 %copy-start.4 = (bf16[2,1536,128]{2,1,0:T(8,128)(2,1)}, bf16[2,1536,128]{2,1,0:T(8,128)(2,1)S(1)}, u32[]{:S(2)}) copy-start(bf16[2,1536,128]{2,1,0:T(8,128)(2,1)S(1)} %constant_dynamic-update-slice_fusion.refs_4_) | copy-start | bytes 2359300
  52.7 65.0 %collective-permute-start.8 = (bf16[2,1536,128]{2,1,0:T(8,128)(2,1)S(1)}, bf16[2,1536,128]{2,1,0:T(8,128)(2,1)S(1)}, u32[]{:S(2)}, u32[]{:S(2)}) collective-permute-start(bf16[2,1536,128]{2,1,0:T(8,128)(2,1)S(1)} %constant_dynamic-update-slice_fusion.refs_4_), channel_id=1, source_target_pairs={{6,0},{0,2},{2,4},{4,6},{7,1},{1,3},{3,5},{5,7},{14,8},{8,10},{10,... | collective-permute-start | bytes 2359304 | tf_op jit(solution)/shard_map/ppermute | solution.py:196
  54.6 21.4 %collective-permute-start.9 = (bf16[1,1536,128]{2,1,0:T(8,128)(2,1)S(1)}, bf16[1,1536,128]{2,1,0:T(8,128)(2,1)S(1)}, u32[]{:S(2)}, u32[]{:S(2)}) collective-permute-start(bf16[1,1536,128]{2,1,0:T(8,128)(2,1)S(1)} %copy-done.5), channel_id=1, source_target_pairs={{16,0},{24,8},{0,16},{8,24},{17,1},{25,9},{1,17},{9,25},{18,2},{26... | collective-permute-start | bytes 1179656 | tf_op jit(solution)/shard_map/ppermute | solution.py:196
  58.9 67.1 %collective-permute-start.7 = (bf16[2,1536,128]{2,1,0:T(8,128)(2,1)S(1)}, bf16[2,1536,128]{2,1,0:T(8,128)(2,1)S(1)}, u32[]{:S(2)}, u32[]{:S(2)}) collective-permute-start(bf16[2,1536,128]{2,1,0:T(8,128)(2,1)S(1)} %constant_dynamic-update-slice_fusion.refs_4_), channel_id=1, source_target_pairs={{2,0},{4,2},{6,4},{0,6},{3,1},{5,3},{7,5},{1,7},{10,8},{12,10},{14... | collective-permute-start | bytes 2359304 | tf_op jit(solution)/shard_map/ppermute | solution.py:196
  62.3 44.1 %collective-permute-start.2 = (bf16[1,1536,128]{2,1,0:T(8,128)(2,1)S(1)}, bf16[1,1536,128]{2,1,0:T(8,128)(2,1)S(1)}, u32[]{:S(2)}, u32[]{:S(2)}) collective-permute-start(bf16[1,1536,128]{2,1,0:T(8,128)(2,1)S(1)} %copy-done.5), channel_id=1, source_target_pairs={{2,0},{4,2},{6,4},{0,6},{3,1},{5,3},{7,5},{1,7},{10,8},{12,10},{14... | collective-permute-start | bytes 1179656 | tf_op jit(solution)/shard_map/ppermute | solution.py:196
  65.5 91.5 %collective-permute-start.1 = (bf16[8,520,128]{2,1,0:T(8,128)(2,1)}, bf16[8,520,128]{2,1,0:T(8,128)(2,1)S(1)}, u32[]{:S(2)}, u32[]{:S(2)}) collective-permute-start(bf16[8,520,128]{2,1,0:T(8,128)(2,1)} %all-to-all-done), channel_id=1, source_target_pairs={{256,0},{0,256},{257,1},{1,257},{258,2},{2,258},{259,3},{3,259},{2... | collective-permute-start | bytes 3194888 | tf_op jit(solution)/shard_map/ppermute | solution.py:251
  76.1 67.8 %copy-start.6 = (bf16[1,1536,128]{2,1,0:T(8,128)(2,1)}, bf16[1,1536,128]{2,1,0:T(8,128)(2,1)S(1)}, u32[]{:S(2)}) copy-start(bf16[1,1536,128]{2,1,0:T(8,128)(2,1)S(1)} %collective-permute-done.9.refs_7_) | copy-start | bytes 1179652
  76.1 43.6 %collective-permute-start.11 = (bf16[1,1536,128]{2,1,0:T(8,128)(2,1)S(1)}, bf16[1,1536,128]{2,1,0:T(8,128)(2,1)S(1)}, u32[]{:S(2)}, u32[]{:S(2)}) collective-permute-start(bf16[1,1536,128]{2,1,0:T(8,128)(2,1)S(1)} %collective-permute-done.9.refs_7_), channel_id=1, source_target_pairs={{6,0},{0,2},{2,4},{4,6},{7,1},{1,3},{3,5},{5,7},{14,8},{8,10},{10,... | collective-permute-start | bytes 1179656 | tf_op jit(solution)/shard_map/ppermute | solution.py:196
  106.4 37.4 %copy-start.7 = (bf16[1,1536,128]{2,1,0:T(8,128)(2,1)}, bf16[1,1536,128]{2,1,0:T(8,128)(2,1)S(1)}, u32[]{:S(2)}) copy-start(bf16[1,1536,128]{2,1,0:T(8,128)(2,1)S(1)} %collective-permute-done.2.refs_1_) | copy-start | bytes 1179652
  106.5 21.6 %collective-permute-start.3 = (bf16[1,1536,128]{2,1,0:T(8,128)(2,1)S(1)}, bf16[1,1536,128]{2,1,0:T(8,128)(2,1)S(1)}, u32[]{:S(2)}, u32[]{:S(2)}) collective-permute-start(bf16[1,1536,128]{2,1,0:T(8,128)(2,1)S(1)} %copy-done.5), channel_id=1, source_target_pairs={{6,0},{0,2},{2,4},{4,6},{7,1},{1,3},{3,5},{5,7},{14,8},{8,10},{10,... | collective-permute-start | bytes 1179656 | tf_op jit(solution)/shard_map/ppermute | solution.py:196
  117.7 26.3 %copy-start.2 = (bf16[2,1536,128]{2,1,0:T(8,128)(2,1)}, bf16[2,1536,128]{2,1,0:T(8,128)(2,1)S(1)}, u32[]{:S(2)}) copy-start(bf16[2,1536,128]{2,1,0:T(8,128)(2,1)S(1)} %collective-permute-done.8.refs_6_) | copy-start | bytes 2359300
  117.7 15.2 %collective-permute-start.10 = (bf16[1,1536,128]{2,1,0:T(8,128)(2,1)S(1)}, bf16[1,1536,128]{2,1,0:T(8,128)(2,1)S(1)}, u32[]{:S(2)}, u32[]{:S(2)}) collective-permute-start(bf16[1,1536,128]{2,1,0:T(8,128)(2,1)S(1)} %collective-permute-done.9.refs_7_), channel_id=1, source_target_pairs={{2,0},{4,2},{6,4},{0,6},{3,1},{5,3},{7,5},{1,7},{10,8},{12,10},{14... | collective-permute-start | bytes 1179656 | tf_op jit(solution)/shard_map/ppermute | solution.py:196
  119.6 24.2 %copy-start.8 = (bf16[1,1536,128]{2,1,0:T(8,128)(2,1)}, bf16[1,1536,128]{2,1,0:T(8,128)(2,1)S(1)}, u32[]{:S(2)}) copy-start(bf16[1,1536,128]{2,1,0:T(8,128)(2,1)S(1)} %collective-permute-done.11.refs_9_) | copy-start | bytes 1179652
  119.7 16.8 %collective-permute-start.4 = (bf16[1,1536,128]{2,1,0:T(8,128)(2,1)S(1)}, bf16[1,1536,128]{2,1,0:T(8,128)(2,1)S(1)}, u32[]{:S(2)}, u32[]{:S(2)}) collective-permute-start(bf16[1,1536,128]{2,1,0:T(8,128)(2,1)S(1)} %collective-permute-done.2.refs_1_), channel_id=1, source_target_pairs={{2,0},{4,2},{6,4},{0,6},{3,1},{5,3},{7,5},{1,7},{10,8},{12,10},{14... | collective-permute-start | bytes 1179656 | tf_op jit(solution)/shard_map/ppermute | solution.py:196
  126.0 17.9 %copy-start.3 = (bf16[2,1536,128]{2,1,0:T(8,128)(2,1)}, bf16[2,1536,128]{2,1,0:T(8,128)(2,1)S(1)}, u32[]{:S(2)}) copy-start(bf16[2,1536,128]{2,1,0:T(8,128)(2,1)S(1)} %collective-permute-done.7.refs_5_) | copy-start | bytes 2359300
  126.0 10.4 %collective-permute-start.14 = (bf16[1,1536,128]{2,1,0:T(8,128)(2,1)S(1)}, bf16[1,1536,128]{2,1,0:T(8,128)(2,1)S(1)}, u32[]{:S(2)}, u32[]{:S(2)}) collective-permute-start(bf16[1,1536,128]{2,1,0:T(8,128)(2,1)S(1)} %collective-permute-done.11.refs_9_), channel_id=1, source_target_pairs={{6,0},{0,2},{2,4},{4,6},{7,1},{1,3},{3,5},{5,7},{14,8},{8,10},{10,... | collective-permute-start | bytes 1179656 | tf_op jit(solution)/shard_map/ppermute | solution.py:196
  128.0 15.9 %copy-start.9 = (bf16[1,1536,128]{2,1,0:T(8,128)(2,1)}, bf16[1,1536,128]{2,1,0:T(8,128)(2,1)S(1)}, u32[]{:S(2)}) copy-start(bf16[1,1536,128]{2,1,0:T(8,128)(2,1)S(1)} %collective-permute-done.3.refs_2_) | copy-start | bytes 1179652
  128.0 15.8 %collective-permute-start.13 = (bf16[1,1536,128]{2,1,0:T(8,128)(2,1)S(1)}, bf16[1,1536,128]{2,1,0:T(8,128)(2,1)S(1)}, u32[]{:S(2)}, u32[]{:S(2)}) collective-permute-start(bf16[1,1536,128]{2,1,0:T(8,128)(2,1)S(1)} %slice.17), channel_id=1, source_target_pairs={{6,0},{0,2},{2,4},{4,6},{7,1},{1,3},{3,5},{5,7},{14,8},{8,10},{10,... | collective-permute-start | bytes 1179656 | tf_op jit(solution)/shard_map/ppermute | solution.py:196
  132.8 11.1 %copy-start.10 = (bf16[1,1536,128]{2,1,0:T(8,128)(2,1)}, bf16[1,1536,128]{2,1,0:T(8,128)(2,1)S(1)}, u32[]{:S(2)}) copy-start(bf16[1,1536,128]{2,1,0:T(8,128)(2,1)S(1)} %collective-permute-done.10.refs_8_) | copy-start | bytes 1179652
  132.8 11.1 %collective-permute-start.12 = (bf16[1,1536,128]{2,1,0:T(8,128)(2,1)S(1)}, bf16[1,1536,128]{2,1,0:T(8,128)(2,1)}, u32[]{:S(2)}, u32[]{:S(2)}) collective-permute-start(bf16[1,1536,128]{2,1,0:T(8,128)(2,1)S(1)} %slice.16), channel_id=1, source_target_pairs={{2,0},{4,2},{6,4},{0,6},{3,1},{5,3},{7,5},{1,7},{10,8},{12,10},{14... | collective-permute-start | bytes 1179656 | tf_op jit(solution)/shard_map/ppermute | solution.py:196
  136.4 7.5 %copy-start.11 = (bf16[1,1536,128]{2,1,0:T(8,128)(2,1)}, bf16[1,1536,128]{2,1,0:T(8,128)(2,1)S(1)}, u32[]{:S(2)}) copy-start(bf16[1,1536,128]{2,1,0:T(8,128)(2,1)S(1)} %collective-permute-done.4.refs_3_) | copy-start | bytes 1179652
  136.4 7.5 %copy-start.12 = (bf16[1,1536,128]{2,1,0:T(8,128)(2,1)}, bf16[1,1536,128]{2,1,0:T(8,128)(2,1)S(1)}, u32[]{:S(2)}) copy-start(bf16[1,1536,128]{2,1,0:T(8,128)(2,1)S(1)} %collective-permute-done.14.refs_12_) | copy-start | bytes 1179652
  143.9 0.8 copy-start.13
  149.8 14.3 %collective-permute-start.16 = (f32[128,1536]{1,0:T(8,128)S(1)}, f32[128,1536]{1,0:T(8,128)S(1)}, u32[]{:S(2)}, u32[]{:S(2)}) collective-permute-start(f32[128,1536]{1,0:T(8,128)S(1)} %get-tuple-element.13), channel_id=1, source_target_pairs={{1,0},{0,1},{3,2},{2,3},{5,4},{4,5},{7,6},{6,7},{9,8},{8,9},{11,10... | collective-permute-start | bytes 2359304 | tf_op jit(solution)/shard_map/ppermute | solution.py:297
  157.0 7.2 %copy-start = (bf16[1,1,256,3072]{3,2,1,0:T(8,128)(2,1)S(1)}, bf16[1,1,256,3072]{3,2,1,0:T(8,128)(2,1)}, u32[]{:S(2)}) copy-start(bf16[1,1,256,3072]{3,2,1,0:T(8,128)(2,1)} %param.8) | copy-start | bytes 4718596
  162.2 9.0 %collective-permute-start.15 = (f32[128,1536]{1,0:T(8,128)S(1)}, f32[128,1536]{1,0:T(8,128)S(1)}, u32[]{:S(2)}, u32[]{:S(2)}) collective-permute-start(f32[128,1536]{1,0:T(8,128)S(1)} %shard_map.71), channel_id=1, source_target_pairs={{1,0},{0,1},{3,2},{2,3},{5,4},{4,5},{7,6},{6,7},{9,8},{8,9},{11,10... | collective-permute-start | bytes 2359304 | tf_op jit(solution)/shard_map/ppermute | solution.py:297
  171.2 39.1 %copy-start.1 = (s32[128,8]{0,1:T(8,128)S(1)}, s32[128,8]{0,1:T(8,128)}, u32[]{:S(2)}) copy-start(s32[128,8]{0,1:T(8,128)} %param.6) | copy-start | bytes 12292
